TPU v7x, 256 devices: a whole 4x4x8 slice. The times are simulated.
256 devices in a mesh: query: 4 (over y), cluster: 64 (over x, z, core).
Axes of the slice: x: 4, y: 4, z: 8, core: 2. Of those that a mesh axis runs over, the one named last changes fastest.
Arguments:
- queries: bfloat16 [1024, 512], P(('query', 'cluster')), may hold values from -68 to 68
- centroids: bfloat16 [512, 512], P('cluster'), may hold values from -6 to 6
- leaves: bfloat16 [512, 1024, 512], P('cluster'), may hold values from -5 to 5
- beam: int32 [1024, 8], P('query'), may hold values from 0 to 511, all different within a row; in each aligned block of 256 rows (0 to 255, 256 to 511, ...) at most 8 rows name the same one
Outputs:
- readout: bfloat16 [1024, 512], P(('query', 'cluster'))
- beam_logprob: float32 [1024, 8], P(('query', 'cluster'))
Inputs may be any that keep to these rules, and one draw needn't show every extreme that they name: `beam`: each row names 8 different clusters. In each aligned block of 256 rows (the queries of one index of query) no cluster is named by more than 8 rows, a bound that some block reaches.
All inputs are finite; a program needn't handle non-finite values.
Results may differ from a plain program's by a relative error of at most 0.0028.
Values may be sent and summed in bfloat16 or wider, within the bound.
No kernel may reach another device: no remote copies, remote signals or barrier semaphores. Data moves between devices by JAX's collectives and lax.ppermute only.
A program may use at most 128 MiB of HBM per device.

v0:
```python
import math

import jax
import jax.numpy as jnp
from jax import lax
from jax.sharding import PartitionSpec as P

floor_value = -1e30


def merged_2(part, axis, combine):
    gathered = jax.tree.map(lambda a: lax.all_gather(a, axis), part)

    def take(source):
        return jax.tree.map(lambda a: lax.dynamic_index_in_dim(a, source, 0, False), gathered)

    return lax.fori_loop(
        1, lax.axis_size(axis), lambda source, state: combine(state, take(source)), take(0)
    )


def combine_states(first, second):
    cmax_one, csum_one, beam_one, lmax_one, lsum_one, accum_one = first
    cmax_two, csum_two, beam_two, lmax_two, lsum_two, accum_two = second
    cmax_new = jnp.maximum(cmax_one, cmax_two)
    csum_new = csum_one * jnp.exp(cmax_one - cmax_new) + csum_two * jnp.exp(cmax_two - cmax_new)
    lmax_new = jnp.maximum(lmax_one, lmax_two)
    factor_one = jnp.exp(lmax_one - lmax_new)
    factor_two = jnp.exp(lmax_two - lmax_new)
    lsum_new = lsum_one * factor_one + lsum_two * factor_two
    accum_new = accum_one * factor_one[:, None] + accum_two * factor_two[:, None]
    return (cmax_new, csum_new, beam_one + beam_two, lmax_new, lsum_new, accum_new)


def per_device(queries, centroids, leaves, beam):
    groups = lax.axis_size("cluster")
    query_block = lax.all_gather(queries, "cluster", axis=0, tiled=True)
    query_count, model_width = query_block.shape
    cluster_count, leaf_count, unused_width = leaves.shape
    beam_width = beam.shape[1]
    score_scale = 1.0 / math.sqrt(model_width)
    first_cluster = lax.axis_index("cluster") * cluster_count
    cscore = jnp.dot(query_block, centroids.T, preferred_element_type=jnp.float32) * score_scale
    cmax_part = jnp.max(cscore, axis=1)
    csum_part = jnp.sum(jnp.exp(cscore - cmax_part[:, None]), axis=1)
    owned = first_cluster + jnp.arange(cluster_count, dtype=jnp.int32)
    matches = beam[:, :, None] == owned[None, None, :]
    beam_part = jnp.sum(jnp.where(matches, cscore[:, None, :], 0.0), axis=2)
    membership = jnp.any(matches, axis=1).astype(jnp.int32)
    slot_index = jnp.cumsum(membership, axis=0) - 1
    capacity = max(4, 2 * query_count * beam_width // (cluster_count * groups))
    positions = jnp.arange(capacity, dtype=jnp.int32)
    dispatch = (membership.T[:, None, :] == 1) & (
        slot_index.T[:, None, :] == positions[None, :, None]
    )
    picked = jnp.einsum(
        "csq,qd->csd",
        dispatch.astype(jnp.bfloat16),
        query_block,
        preferred_element_type=jnp.float32,
    ).astype(jnp.bfloat16)
    slot_centroid = jnp.sum(jnp.where(dispatch, cscore.T[:, None, :], 0.0), axis=2)
    logits = (
        jnp.einsum("csd,cjd->csj", picked, leaves, preferred_element_type=jnp.float32) * score_scale
    )
    logits = logits + slot_centroid[:, :, None]
    slot_max = jnp.max(logits, axis=2)
    weights = jnp.exp(logits - slot_max[:, :, None])
    slot_sum = jnp.sum(weights, axis=2)
    slot_accum = jnp.einsum(
        "csj,cjd->csd", weights.astype(jnp.bfloat16), leaves, preferred_element_type=jnp.float32
    )
    slot_total = cluster_count * capacity
    dispatch_flat = dispatch.reshape(slot_total, query_count)
    slot_max_flat = slot_max.reshape(slot_total)
    masked_max = jnp.where(dispatch_flat, slot_max_flat[:, None], floor_value)
    lmax_part = jnp.max(masked_max, axis=0)
    exponent = jnp.where(dispatch_flat, slot_max_flat[:, None] - lmax_part[None, :], 0.0)
    factors = jnp.where(dispatch_flat, jnp.exp(exponent), 0.0)
    lsum_part = jnp.sum(factors * slot_sum.reshape(slot_total)[:, None], axis=0)
    accum_part = jnp.dot(
        factors.T,
        slot_accum.reshape(slot_total, model_width),
        precision=lax.Precision.HIGHEST,
        preferred_element_type=jnp.float32,
    )
    state = (cmax_part, csum_part, beam_part, lmax_part, lsum_part, accum_part)
    row_count = query_count // groups
    merged = merged_2(state, "cluster", combine_states)
    row_start = lax.axis_index("cluster") * row_count
    own = tuple((lax.dynamic_slice_in_dim(member, row_start, row_count, 0) for member in merged))
    cmax_own, csum_own, beam_own, lmax_own, lsum_own, accum_own = own
    lse = cmax_own + jnp.log(csum_own)
    beam_logprob = beam_own - lse[:, None]
    readout = (accum_own / lsum_own[:, None]).astype(jnp.bfloat16)
    return (readout, beam_logprob)


def solution(mesh):
    return jax.shard_map(
        per_device,
        mesh=mesh,
        in_specs=(
            P(("query", "cluster"), None),
            P("cluster", None),
            P("cluster", None, None),
            P("query", None),
        ),
        out_specs=(P(("query", "cluster"), None), P(("query", "cluster"), None)),
        check_vma=False,
    )
```

profile of v0, /device:TPU:32, one launch (start us, length us, event | category | flops | bytes accessed | tf_op | source)
XLA Modules:
  0.0 383.7 jit_solution(5033531399816368670)
XLA Ops:
  8.0 46.5 %all-gather.6 = bf16[64,4,512]{2,1,0:T(4,128)(2,1)S(1)} all-gather(bf16[1,4,512]{2,1,0:T(4,128)(2,1)} %bitcast.79), channel_id=1, replica_groups=mesh['query'=4,'cluster'=64] {'cluster'}, dimensions={0}, use_global_device_ids=true | all-gather | bytes 266240 | tf_op jit(solution)/shard_map/all_gather | solution.py:37
  55.9 5.8 %fusion.25 = (f32[8,8]{1,0:T(8,128)S(1)}, f32[8,8,1024]{2,1,0:T(8,128)S(1)}) fusion(f32[8,8]{1,0:T(8,128)S(1)} %select_reduce_fusion.1, bf16[8,1024,512]{2,1,0:T(8,128)(2,1)} %param.8, bf16[256,512,1]{1,0,2:T(8,128)(2,1)S(1)} %reshape.124, s32[8,256]{1,0:T(8,128)S(1)} %add_bitcast_fusion, pred[8,256]{1,0:T(8,128)(4,1)S(1)} %fusion.21), kind=kOutput, calls=%fused_computation.54 | convolution fusion | flops 84148160 | bytes 8923648 | tf_op jit(solution)/shard_map/csd,cjd->csj/dot_general | solution.py:64
  61.8 4.6 %fusion.4 = f32[8,8,512]{2,1,0:T(8,128)S(1)} fusion(bf16[8,1024,512]{2,1,0:T(8,128)(2,1)} %param.8, f32[8,8,1024]{2,1,0:T(8,128)S(1)} %get-tuple-element.358, f32[8,8]{1,0:T(8,128)S(1)} %get-tuple-element.357), kind=kOutput, calls=%fused_computation.19 | convolution fusion | flops 67239936 | bytes 8782080 | tf_op jit(solution)/shard_map/csj,cjd->csd/dot_general | solution.py:70
  66.4 1.5 convolution_bitcast_fusion
  68.3 41.6 %all-gather.10 = f32[64,1,256]{2,1,0:T(1,128)S(1)} all-gather(f32[1,1,256]{2,1,0:T(1,128)S(1)} %bitcast.82), channel_id=6, replica_groups=mesh['query'=4,'cluster'=64] {'cluster'}, dimensions={0}, use_global_device_ids=true | all-gather | bytes 66560 | tf_op jit(solution)/shard_map/all_gather | solution.py:12
  109.9 43.8 %all-gather.8 = f32[64,1,256]{2,1,0:T(1,128)S(1)} all-gather(f32[1,1,256]{2,1,0:T(1,128)S(1)} %bitcast.80), channel_id=3, replica_groups=mesh['query'=4,'cluster'=64] {'cluster'}, dimensions={0}, use_global_device_ids=true | all-gather | bytes 66560 | tf_op jit(solution)/shard_map/all_gather | solution.py:12
  153.7 43.8 %all-gather.9 = f32[64,1,256]{2,1,0:T(1,128)S(1)} all-gather(f32[1,1,256]{2,1,0:T(1,128)S(1)} %bitcast.81), channel_id=5, replica_groups=mesh['query'=4,'cluster'=64] {'cluster'}, dimensions={0}, use_global_device_ids=true | all-gather | bytes 66560 | tf_op jit(solution)/shard_map/all_gather | solution.py:12
  197.6 42.8 %all-gather.7 = f32[64,1,256]{2,1,0:T(1,128)S(1)} all-gather(f32[1,1,256]{2,1,0:T(1,128)S(1)} %bitcast.78), channel_id=2, replica_groups=mesh['query'=4,'cluster'=64] {'cluster'}, dimensions={0}, use_global_device_ids=true | all-gather | bytes 66560 | tf_op jit(solution)/shard_map/all_gather | solution.py:12
  240.5 48.5 %all-gather.2 = f32[16384,8]{0,1:T(8,128)S(1)} all-gather(f32[256,8]{0,1:T(8,128)S(1)} %fusion.7), channel_id=4, replica_groups=mesh['query'=4,'cluster'=64] {'cluster'}, dimensions={0}, use_global_device_ids=true | all-gather | bytes 532480 | tf_op jit(solution)/shard_map/all_gather | solution.py:12
  290.0 85.2 %while.25 = (s32[]{:T(128)}, f32[256]{0:T(256)S(1)}, f32[256]{0:T(256)S(1)}, f32[256,8]{0,1:T(8,128)S(1)}, f32[256]{0:T(256)S(1)}, /*index=5*/f32[256]{0:T(256)S...) while((s32[]{:T(128)}, f32[256]{0:T(256)S(1)}, ...), condition=%wide.region_12.13_spmd, body=%wide.region_11.12_spmd.sunk | while | flops 398341 | bytes 1622215 | solution.py:17
  290.1 1.2 fusion.35
  294.2 1.2 fusion.35
  295.6 1.2 fusion.35
  296.9 1.2 fusion.35
  298.3 1.2 fusion.35
  299.6 1.2 fusion.35
  301.0 1.2 fusion.35
  302.3 1.2 fusion.35
  307.7 1.2 fusion.35
  309.1 1.2 fusion.35
  310.4 1.2 fusion.35
  311.8 1.2 fusion.35
  313.1 1.2 fusion.35
  314.5 1.2 fusion.35
  (404 shorter events, 70.2 us)
Async XLA Ops:
  7.2 48.4 %copy-start = (bf16[8,512]{1,0:T(8,128)(2,1)S(1)}, bf16[8,512]{1,0:T(8,128)(2,1)}, u32[]{:S(2)}) copy-start(bf16[8,512]{1,0:T(8,128)(2,1)} %param.7) | copy-start | bytes 24580
  7.2 281.8 %all-gather.13.cloned.1.call-start = ((), (), s32[]{:S(2)}) async-start(), calls=%async_computation | async-start | bytes 34078720 | tf_op jit(solution)/shard_map/all_gather | solution.py:12
  61.7 178.6 %copy-start.1 = (s32[256,8]{0,1:T(8,128)S(1)}, s32[256,8]{0,1:T(8,128)}, u32[]{:S(2)}) copy-start(s32[256,8]{0,1:T(8,128)} %param.9) | copy-start | bytes 24580
Sparse Core Ops, SparseCore 0:
  68.1 138.4 all-gather.12
where the time goes:
time: 390 us; the launch traced here: 384 us
  blocking collectives  267 us (68%)
  other arithmetic  84.1 us (22%)
  between operations  14.1 us (4%)
  matrix products  12.1 us (3%)
    all_gather x5, blocking collectives, merged_2(): gathered = jax.tree.map(lambda a: lax.all_gather(a, axis), part)  221 us
    add x63, other arithmetic, combine_states(): accum_one * factor_one[:, None] + accum_two * factor_two[:, None]  77.4 us
    all_gather x1, blocking collectives, per_device(): query_block = lax.all_gather(queries, 'cluster', axis=0, tiled=True)  46.5 us
  transfers between devices with their start and end apart: 1, of which 0 were waited for; matrix products, arithmetic and copies ran while one was open for 0% of the time, Pallas kernels for 0%

commit v1 on v0

v1 whole, which is shorter than its diff:
```python
import math

import jax
import jax.numpy as jnp
from jax import lax
from jax.sharding import PartitionSpec as P

floor_value = -1e30


def combine(first, second):
    m1, l1, a1 = first
    m2, l2, a2 = second
    m = jnp.maximum(m1, m2)
    f1 = jnp.exp(m1 - m)
    f2 = jnp.exp(m2 - m)
    return m, f1 * l1 + f2 * l2, f1 * a1 + f2 * a2


def per_device(queries, centroids, leaves, beam):
    groups = lax.axis_size("cluster")
    rows, width = queries.shape
    count, leaf_count, _ = leaves.shape
    top = beam.shape[1]
    pairs = groups // 2
    half = pairs * rows
    total = 2 * half
    scale = 1.0 / math.sqrt(width)
    me = lax.axis_index("cluster")
    side = me % 2
    sides = [[2 * i + c for i in range(pairs)] for c in range(2)]
    swap = [(i, i ^ 1) for i in range(groups)]

    own_q = lax.all_to_all(
        jnp.broadcast_to(queries[None], (pairs, rows, width)), "cluster", 0, 0, axis_index_groups=sides
    )
    other_q = lax.ppermute(own_q, "cluster", swap)
    q = jnp.concatenate([own_q, other_q], axis=0).reshape(total, width)
    beams = beam.reshape(pairs, 2, rows, top)
    b0 = beams[:, 0].reshape(half, top)
    b1 = beams[:, 1].reshape(half, top)
    own_beam = jnp.where(side == 0, b0, b1)
    b = jnp.concatenate([own_beam, jnp.where(side == 0, b1, b0)], axis=0)

    cscore = jnp.dot(q, centroids.T, preferred_element_type=jnp.float32) * scale
    owned = me * count + jnp.arange(count, dtype=jnp.int32)
    member = jnp.any(b[:, :, None] == owned[None, None, :], axis=1)
    rank = jnp.dot(
        jnp.tril(jnp.ones((total, total), jnp.bfloat16)),
        member.astype(jnp.bfloat16),
        preferred_element_type=jnp.float32,
    )
    capacity = 8
    slots = jnp.arange(1, capacity + 1, dtype=jnp.float32)
    dispatch = member.T[:, None, :] & (rank.T[:, None, :] == slots[None, :, None])
    picked = jnp.einsum(
        "csq,qd->csd", dispatch.astype(jnp.bfloat16), q, preferred_element_type=jnp.float32
    ).astype(jnp.bfloat16)
    slot_c = jnp.sum(jnp.where(dispatch, cscore.T[:, None, :], 0.0), axis=2)
    logits = jnp.einsum("csd,cjd->csj", picked, leaves, preferred_element_type=jnp.float32) * scale
    logits = logits + slot_c[:, :, None]
    slot_m = jnp.max(logits, axis=2)
    w = jnp.exp(logits - slot_m[:, :, None])
    slot_l = jnp.sum(w, axis=2)
    slot_a = jnp.einsum(
        "csj,cjd->csd", w.astype(jnp.bfloat16), leaves, preferred_element_type=jnp.float32
    )
    n = count * capacity
    d2 = dispatch.reshape(n, total)
    mm = slot_m.reshape(n, 1)
    m = jnp.max(jnp.where(d2, mm, floor_value), axis=0)
    f = jnp.where(d2, jnp.exp(jnp.where(d2, mm - m[None, :], 0.0)), 0.0)
    l = jnp.sum(f * slot_l.reshape(n, 1), axis=0)
    acc = lax.dot_general(
        f,
        slot_a.reshape(n, width),
        (((0,), (0,)), ((), ())),
        precision=lax.Precision.HIGHEST,
        preferred_element_type=jnp.float32,
    )
    pad = jnp.zeros((total, 128 - count - 2), jnp.float32)
    state = jnp.concatenate([acc, m[:, None], l[:, None], cscore, pad], axis=1)
    mine, theirs = state[:half], lax.ppermute(state[half:], "cluster", swap)

    def parts(s):
        return s[:, width : width + 1], s[:, width + 1 : width + 2], s[:, :width]

    m, l, acc = combine(parts(mine), parts(theirs))
    cs = slice(width + 2, width + 2 + count)
    pad = jnp.zeros((half, 128 - 2 * count - 2), jnp.float32)
    state = jnp.concatenate([acc, m, l, mine[:, cs], theirs[:, cs], pad], axis=1)
    got = lax.all_to_all(
        state.reshape(pairs, rows, width + 128), "cluster", 0, 0, axis_index_groups=sides
    )
    acc, m, l = got[:, :, :width], got[:, :, width], got[:, :, width + 1]
    scores = got[:, :, width + 2 : width + 2 + 2 * count]
    top_m = jnp.max(m, axis=0)
    f = jnp.exp(m - top_m[None])
    readout = jnp.sum(f[:, :, None] * acc, axis=0) / jnp.sum(f * l, axis=0)[:, None]
    cmax = jnp.max(scores, axis=(0, 2))
    lse = cmax + jnp.log(jnp.sum(jnp.exp(scores - cmax[None, :, None]), axis=(0, 2)))
    j = jnp.arange(2 * count, dtype=jnp.int32)
    from_side = jnp.where(j < count, side, 1 - side)
    ids = (2 * jnp.arange(pairs, dtype=jnp.int32)[:, None] + from_side[None]) * count + j[None] % count
    chip = me // 2
    my_beam = lax.dynamic_slice_in_dim(own_beam, chip * rows, rows, 0)
    hit = my_beam[None, :, :, None] == ids[:, None, None, :]
    picked_score = jnp.sum(jnp.where(hit, scores[:, :, None, :], 0.0), axis=(0, 3))
    return readout.astype(jnp.bfloat16), picked_score - lse[:, None]


def solution(mesh):
    return jax.shard_map(
        per_device,
        mesh=mesh,
        in_specs=(
            P(("query", "cluster"), None),
            P("cluster", None),
            P("cluster", None, None),
            P("query", None),
        ),
        out_specs=(P(("query", "cluster"), None), P(("query", "cluster"), None)),
        check_vma=False,
    )
```

time: 390 us -> 62.4 us (0.16); the launches traced: 384 us -> 62 us
  blocking collectives: 267 us -> 0 us
  other arithmetic: 84.1 us -> 2.82 us
  waiting for transfers between devices: 0.02 us -> 25.5 us
  starting transfers between devices: 0.04 us -> 15.7 us
  between operations: 14.1 us -> 0.9 us
    all_gather x6 -> x0, blocking collectives: 267 us -> none  [the longest x5 221 us: merged_2(): gathered = jax.tree.map(lambda a: lax.all_gather(a, axis), part)]
    add x254 -> x6, other arithmetic: 80.7 us -> 0.14 us  [the longest x1 0.07 us: per_device(): (2 * jnp.arange(pairs, dtype=jnp.int32)[:, None] + from_side[None]) * count]
    all_to_all x0 -> x2, waiting for transfers between devices: none -> 22.7 us  [the longest x1 14.1 us: per_device(): lax.all_to_all(state.reshape(pairs, rows, width + 128), 'cluster', 0, 0,...]
    all_to_all x0 -> x2, starting transfers between devices: none -> 15.5 us  [the longest x1 11.2 us: per_device(): lax.all_to_all(jnp.broadcast_to(queries[None], (pairs, rows, width)), 'cl...]
  transfers between devices with their start and end apart: 1 -> 4, of which waited for: 0 -> 4; matrix products, arithmetic and copies ran while one was open for 0% -> 2% of each run, Pallas kernels for 0% -> 0%
where the time goes in v1:
time: 62.4 us; the launch traced here: 62 us
  waiting for transfers between devices  25.5 us (41%)
  starting transfers between devices  15.7 us (25%)
  matrix products  11.4 us (18%)
  local copies, waits for them, and re-layouts  5.7 us (9%)
  other arithmetic  2.82 us (5%)
  between operations  0.9 us (1%)
    all_to_all x1, waiting for transfers between devices, per_device(): lax.all_to_all(state.reshape(pairs, rows, width + 128), 'cluster', 0, 0,...  14.1 us
    all_to_all x1, starting transfers between devices, per_device(): lax.all_to_all(jnp.broadcast_to(queries[None], (pairs, rows, width)), 'cl...  11.2 us
    all_to_all x1, waiting for transfers between devices, per_device(): lax.all_to_all(jnp.broadcast_to(queries[None], (pairs, rows, width)), 'cl...  8.57 us
    dot_general x1, matrix products, per_device(): jnp.einsum('csd,cjd->csj', picked, leaves, preferred_element_type=jnp.flo...  5.86 us
    dot_general x1, matrix products, per_device(): jnp.einsum('csj,cjd->csd', w.astype(jnp.bfloat16), leaves, preferred_elem...  4.62 us
    all_to_all x1, starting transfers between devices, per_device(): lax.all_to_all(state.reshape(pairs, rows, width + 128), 'cluster', 0, 0,...  4.27 us
    unnamed x7, local copies, waits for them, and re-layouts  1.84 us
    ppermute x1, waiting for transfers between devices, per_device(): mine, theirs = (state[:half], lax.ppermute(state[half:], 'cluster', swap))  1.48 us
  transfers between devices with their start and end apart: 4, of which 4 were waited for; matrix products, arithmetic and copies ran while one was open for 2% of the time, Pallas kernels for 0%

profile of v1, /device:TPU:32, one launch (start us, length us, event | category | flops | bytes accessed | tf_op | source)
XLA Modules:
  0.0 62.0 jit_solution(14576516000975330022)
XLA Ops:
  0.6 1.4 %broadcast_in_dim.92 = bf16[32,4,512]{2,1,0:T(4,128)(2,1)} broadcast(bf16[4,512]{1,0:T(4,128)(2,1)} %param.4), dimensions={1,2} | broadcast | bytes 135168 | tf_op jit(solution)/shard_map/broadcast_in_dim | solution.py:35
  2.0 11.2 %all-to-all-start = ((bf16[32,4,512]{2,1,0:T(4,128)(2,1)}), bf16[32,4,512]{2,1,0:T(4,128)(2,1)S(1)}, u32[]{:S(2)}, u32[]{:S(2)}) async-start(bf16[32,4,512]{2,1,0:T(4,128)(2,1)} %broadcast_in_dim.92), calls=%async_computation | async-start | bytes 262144 | tf_op jit(solution)/shard_map/all_to_all | solution.py:34
  13.2 0.8 %copy.69 = s32[256,8]{1,0:T(8,128)S(1)} copy(s32[256,8]{0,1:T(8,128)} %param.7) | data formatting | bytes 16384 | tf_op args[3]
  14.4 8.6 %all-to-all-done = bf16[32,4,512]{2,1,0:T(4,128)(2,1)S(1)} async-done(((bf16[32,4,512]{2,1,0:T(4,128)(2,1)}), bf16[32,4,512]{2,1,0:T(4,128)(2,1)S(1)}, u32[]{:S(2)}, u32[]{:S(2)}) %all-to-all-start) | async-done | bytes 131104 | tf_op jit(solution)/shard_map/all_to_all | solution.py:34
  23.1 1.3 %collective-permute-done = bf16[32,4,512]{2,1,0:T(4,128)(2,1)S(1)} collective-permute-done((bf16[32,4,512]{2,1,0:T(4,128)(2,1)S(1)}, bf16[32,4,512]{2,1,0:T(4,128)(2,1)S(1)}, u32[]{:S(2)}, u32[]{:S(2)}) %collective-permute-start) | collective-permute-done | bytes 131104 | tf_op jit(solution)/shard_map/ppermute | solution.py:37
  24.7 0.2 select_reduce_fusion.2
  24.9 5.9 %fusion.35 = (f32[8,8]{1,0:T(8,128)S(1)}, f32[8,8,1024]{2,1,0:T(8,128)S(1)}) fusion(f32[8,8]{1,0:T(8,128)S(1)} %select_reduce_fusion.2, bf16[8,1024,512]{2,1,0:T(8,128)(2,1)} %param.6, bf16[256,512,1]{1,0,2:T(8,128)(2,1)S(1)} %reshape.169, f32[8,256]{1,0:T(8,128)S(1)} %fusion.8, f32[8]{0:T(128)S(1)} %iota_add_fusion, pred[8,256]{1,0:T(8,128)(4,1)S(1)} %bitcast.54), kind=kOutput, calls=%fused_computation.72 | convolution fusion | flops 84148160 | bytes 8923680 | tf_op jit(solution)/shard_map/csd,cjd->csj/dot_general | solution.py:60
  30.9 0.2 fusion.4
  31.1 4.6 %fusion.6 = f32[8,8,512]{2,1,0:T(8,128)S(1)} fusion(bf16[8,1024,512]{2,1,0:T(8,128)(2,1)} %param.6, f32[8,8,1024]{2,1,0:T(8,128)S(1)} %get-tuple-element.22, f32[8,8]{1,0:T(8,128)S(1)} %get-tuple-element.21), kind=kOutput, calls=%fused_computation.17 | convolution fusion | flops 67239936 | bytes 8782080 | tf_op jit(solution)/shard_map/csj,cjd->csd/dot_general | solution.py:65
  35.8 0.7 %convolution_bitcast_fusion = f32[256,512]{0,1:T(8,128)S(1)} fusion(f32[8,8,512]{2,1,0:T(8,128)S(1)} %fusion.6, f32[256]{0:T(256)S(1)} %select_reduce_fusion.1, f32[8,8]{1,0:T(8,128)S(1)} %get-tuple-element.21, f32[8,256]{1,0:T(8,128)S(1)} %fusion.8, f32[8]{0:T(128)S(1)} %iota_add_fusion, pred[8,256]{1,0:T(8,128)(4,1)S(1)} %bitcast.57), kind=kOutput, calls=%fused_computation | convolution fusion | flops 100745216 | bytes 666912 | tf_op jit(solution)/shard_map/dot_general | solution.py:74
  36.5 0.5 concatenate.14
  37.0 0.2 collective-permute-start.1
  37.3 1.5 %collective-permute-done.1 = f32[128,640]{0,1:T(8,128)S(1)} collective-permute-done((f32[128,640]{0,1:T(8,128)S(1)}, f32[128,640]{0,1:T(8,128)S(1)}, u32[]{:S(2)}, u32[]{:S(2)}) %collective-permute-start.1) | collective-permute-done | bytes 327712 | tf_op jit(solution)/shard_map/ppermute | solution.py:83
  38.8 0.5 concatenate.15
  39.5 0.8 %reshape.168 = f32[32,4,640]{2,1,0:T(4,128)} reshape(f32[128,640]{1,0:T(8,128)S(1)} %copy.73) | data formatting | bytes 655360 | tf_op jit(solution)/shard_map/reshape | solution.py:93
  40.3 4.3 %all-to-all-start.1 = ((f32[32,4,640]{2,1,0:T(4,128)}), f32[32,4,640]{2,1,0:T(4,128)S(1)}, u32[]{:S(2)}, u32[]{:S(2)}) async-start(f32[32,4,640]{2,1,0:T(4,128)} %reshape.168), calls=%async_computation.1 | async-start | bytes 655360 | tf_op jit(solution)/shard_map/all_to_all | solution.py:92
  44.7 14.1 %all-to-all-done.1 = f32[32,4,640]{2,1,0:T(4,128)S(1)} async-done(((f32[32,4,640]{2,1,0:T(4,128)}), f32[32,4,640]{2,1,0:T(4,128)S(1)}, u32[]{:S(2)}, u32[]{:S(2)}) %all-to-all-start.1) | async-done | bytes 327712 | tf_op jit(solution)/shard_map/all_to_all | solution.py:92
  58.8 0.2 slice_reduce_fusion.1
  59.0 0.2 exponential_reduce_fusion
  59.3 0.2 fusion.34
  59.8 0.2 fusion.25
  60.4 0.7 %copy.79 = bf16[4,512]{1,0:T(4,128)(2,1)} copy(bf16[4,512]{0,1:T(8,128)(2,1)S(1)} %divide_convert_fusion) | data formatting | bytes 8192
  61.1 0.2 select_reduce_fusion
  61.4 0.7 %broadcast_subtract_fusion = f32[4,8]{1,0:T(4,128)} fusion(f32[4,8]{1,0:T(4,128)S(1)} %select_reduce_fusion, f32[4]{0:T(128)S(1)} %log_add_fusion), kind=kLoop, calls=%fused_computation.51 | loop fusion | flops 32 | bytes 272 | tf_op jit(solution)/shard_map/sub | solution.py:109
  (39 shorter events, 2.1 us)
Async XLA Ops:
  0.6 23.9 %copy-start = (bf16[8,512]{1,0:T(8,128)(2,1)S(1)}, bf16[8,512]{1,0:T(8,128)(2,1)}, u32[]{:S(2)}) copy-start(bf16[8,512]{1,0:T(8,128)(2,1)} %param.5) | copy-start | bytes 24580
  2.0 21.0 %all-to-all-start = ((bf16[32,4,512]{2,1,0:T(4,128)(2,1)}), bf16[32,4,512]{2,1,0:T(4,128)(2,1)S(1)}, u32[]{:S(2)}, u32[]{:S(2)}) async-start(bf16[32,4,512]{2,1,0:T(4,128)(2,1)} %broadcast_in_dim.92), calls=%async_computation | async-start | bytes 262144 | tf_op jit(solution)/shard_map/all_to_all | solution.py:34
  23.0 1.3 %collective-permute-start = (bf16[32,4,512]{2,1,0:T(4,128)(2,1)S(1)}, bf16[32,4,512]{2,1,0:T(4,128)(2,1)S(1)}, u32[]{:S(2)}, u32[]{:S(2)}) collective-permute-start(bf16[32,4,512]{2,1,0:T(4,128)(2,1)S(1)} %all-to-all-done), channel_id=1, source_target_pairs={{0,1},{1,0},{2,3},{3,2},{4,5},{5,4},{6,7},{7,6},{8,9},{9,8},{10,11... | collective-permute-start | bytes 393224 | tf_op jit(solution)/shard_map/ppermute | solution.py:37
  37.0 1.7 %collective-permute-start.1 = (f32[128,640]{0,1:T(8,128)S(1)}, f32[128,640]{0,1:T(8,128)S(1)}, u32[]{:S(2)}, u32[]{:S(2)}) collective-permute-start(f32[128,640]{0,1:T(8,128)S(1)} %slice.79), channel_id=1, source_target_pairs={{0,1},{1,0},{2,3},{3,2},{4,5},{5,4},{6,7},{7,6},{8,9},{9,8},{10,11... | collective-permute-start | bytes 983048 | tf_op jit(solution)/shard_map/ppermute | solution.py:83
  40.3 18.5 %all-to-all-start.1 = ((f32[32,4,640]{2,1,0:T(4,128)}), f32[32,4,640]{2,1,0:T(4,128)S(1)}, u32[]{:S(2)}, u32[]{:S(2)}) async-start(f32[32,4,640]{2,1,0:T(4,128)} %reshape.168), calls=%async_computation.1 | async-start | bytes 655360 | tf_op jit(solution)/shard_map/all_to_all | solution.py:92

commit v2 on v1

v2 whole, which is shorter than its diff:
```python
import functools
import math

import jax
import jax.numpy as jnp
from jax import lax
from jax.experimental import pallas as pl
from jax.experimental.pallas import tpu as pltpu
from jax.sharding import PartitionSpec as P

FLOOR = -1e30
CAP = 8
AHEAD = 2
LANES = 128
F32 = jnp.float32
BF16 = jnp.bfloat16


def dot(a, b, ca, cb):
    return lax.dot_general(a, b, (((ca,), (cb,)), ((), ())), preferred_element_type=F32)


def pieces(x):
    hi = x.astype(BF16)
    lo = (x - hi.astype(F32)).astype(BF16)
    return hi, lo


def table_kernel(beam_ref, cent_ref, leaves_ref, disp_ref, disp_t_ref, turned_ref, cent_out, head_out, beam_buf, sems):
    count = cent_ref.shape[0]
    total = beam_ref.shape[1]
    half = total // 2
    rows = total // lax.axis_size("cluster")
    ahead = head_out.shape[0]
    copies = [
        pltpu.make_async_copy(beam_ref, beam_buf, sems.at[0]),
        pltpu.make_async_copy(cent_ref, cent_out, sems.at[1]),
    ] + [pltpu.make_async_copy(leaves_ref.at[c], head_out.at[c], sems.at[2 + c]) for c in range(ahead)]
    for copy in copies:
        copy.start()
    me = lax.axis_index("cluster")
    square = (total, total)
    down, across = (lax.broadcasted_iota(jnp.int32, square, d) for d in range(2))
    upper = jnp.where(down <= across, 1.0, 0.0).astype(BF16)
    r = lax.broadcasted_iota(jnp.int32, (total, 1), 0)
    p, r = r // half, r % half
    source = (r // rows * 2 + (p + me) % 2) * rows + r % rows
    order = jnp.where(source == across, 1.0, 0.0).astype(BF16)
    copies[0].wait()
    beam = beam_buf[...]
    hits = [jnp.max(jnp.where(beam == me * count + c, 1.0, 0.0), axis=0, keepdims=True) for c in range(count)]
    rank = dot(jnp.concatenate(hits, axis=0).astype(BF16), upper, 1, 0)
    slot = lax.broadcasted_iota(jnp.int32, (CAP, total), 0).astype(F32) + 1.0
    disp = jnp.concatenate(
        [jnp.where(slot == rank[c : c + 1], 1.0, 0.0) * hits[c] for c in range(count)], axis=0
    ).astype(BF16)
    disp_ref[...] = dot(disp, order, 1, 1).astype(BF16)
    disp_t_ref[...] = dot(order, disp, 1, 1).astype(BF16)
    coarse = beam // 16 * 16
    halves = jnp.concatenate([coarse, beam - coarse], axis=0).astype(F32).astype(BF16)
    halves = dot(halves, order, 1, 1)
    top = beam.shape[0]
    turned_ref[...] = (halves[:top] + halves[top:]).astype(jnp.int32)
    for copy in copies[1:]:
        copy.wait()


def leaf_kernel(scale, own_ref, other_ref, disp_ref, disp_t_ref, beam_ref, cent_ref, head_ref, leaves_ref, mine_ref, theirs_ref, buf, sems):
    count, leaf_count, width = leaves_ref.shape
    ahead = head_ref.shape[0]
    half = own_ref.shape[0]
    total = 2 * half
    copies = [
        pltpu.make_async_copy(leaves_ref.at[ahead + c], buf.at[c], sems.at[c]) for c in range(count - ahead)
    ]
    for copy in copies:
        copy.start()
    q = jnp.concatenate([own_ref[...], other_ref[...]], axis=0)
    disp = disp_ref[...]
    picked = dot(disp, q, 1, 0).astype(BF16)
    cs = dot(cent_ref[...], q, 1, 1) * scale
    hit = disp.astype(F32)
    cs_wide = jnp.concatenate([jnp.broadcast_to(cs[c : c + 1], (CAP, total)) for c in range(count)], axis=0)
    slot_c = jnp.sum(hit * cs_wide, axis=1, keepdims=True)

    def leaf(c):
        return head_ref[c] if c < ahead else buf[c - ahead]

    def scores(c):
        if c >= ahead:
            copies[c - ahead].wait()
        return dot(picked[c * CAP : (c + 1) * CAP], leaf(c), 1, 1)

    ms, ls, accs = [], [], []
    s = scores(0)
    for c in range(count):
        z = s * scale + slot_c[c * CAP : (c + 1) * CAP]
        if c + 1 < count:
            s = scores(c + 1)
        m = jnp.max(z, axis=1, keepdims=True)
        w = jnp.exp(z - m)
        ms.append(m)
        ls.append(jnp.sum(w, axis=1, keepdims=True))
        accs.append(dot(w.astype(BF16), leaf(c), 1, 0))
    c_m = jnp.max(cs, axis=0, keepdims=True)
    c_l = jnp.sum(jnp.exp(cs - c_m), axis=0, keepdims=True)
    first = lax.axis_index("cluster") * count
    beam = beam_ref[...]
    score = jnp.zeros(beam.shape, F32)
    for c in range(count):
        score = score + jnp.where(beam == first + c, cs[c : c + 1], 0.0)
    m = jnp.concatenate(ms, axis=0)
    l = jnp.concatenate(ls, axis=0)
    acc = jnp.concatenate(accs, axis=0)
    on = hit > 0.5
    q_m = jnp.max(jnp.where(on, m, FLOOR), axis=0, keepdims=True)
    back = jnp.sum(jnp.where(on, q_m, 0.0), axis=1, keepdims=True)
    f = jnp.exp(jnp.minimum(m - back, 0.0))
    q_l = jnp.sum(jnp.where(on, f * l, 0.0), axis=0, keepdims=True)
    hi, lo = pieces(f * acc)
    disp_t = disp_t_ref[...]
    q_acc = dot(disp_t, hi, 1, 0) + dot(disp_t, lo, 1, 0)
    rows = jnp.concatenate([q_m, q_l, c_m, c_l, score, jnp.zeros((4, total), F32)], axis=0)
    for side, ref in enumerate((mine_ref, theirs_ref)):
        for k in range(width // LANES):
            ref[k * half : (k + 1) * half] = q_acc[side * half : (side + 1) * half, k * LANES : (k + 1) * LANES]
        ref[width // LANES * half :] = rows[:, side * half : (side + 1) * half]


def merge_kernel(mine_ref, theirs_ref, out_ref):
    chunks = (mine_ref.shape[0] - 16) // LANES
    half = LANES
    base = chunks * half
    a, b = mine_ref[base : base + 16], theirs_ref[base : base + 16]
    m = jnp.maximum(a[0:1], b[0:1])
    fa, fb = jnp.exp(a[0:1] - m), jnp.exp(b[0:1] - m)
    l = fa * a[1:2] + fb * b[1:2]
    c = jnp.maximum(a[2:3], b[2:3])
    cl = jnp.exp(a[2:3] - c) * a[3:4] + jnp.exp(b[2:3] - c) * b[3:4]
    block = jnp.concatenate([m, l, c, cl, a[4:12] + b[4:12], fa, fb, jnp.zeros((LANES - 14, half), F32)], axis=0)
    cols = block.T
    fa, fb = cols[:, 12:13], cols[:, 13:14]
    per = out_ref.shape[0] * 4 // half
    outs = [
        fa * mine_ref[k * half : (k + 1) * half] + fb * theirs_ref[k * half : (k + 1) * half] for k in range(chunks)
    ] + [cols]
    for k, value in enumerate(outs):
        for d in range(half // 4):
            out_ref[per * d + k] = value[4 * d : 4 * d + 4]


def home_kernel(got_ref, readout_ref, logprob_ref):
    rows, width = readout_ref.shape
    chunks = width // LANES
    per = chunks + 1
    pairs = got_ref.shape[0] // per
    info = [got_ref[per * d + chunks] for d in range(pairs)]
    top = functools.reduce(jnp.maximum, info)
    total = functools.reduce(jnp.add, info)
    factors = [jnp.exp(x - top) for x in info]
    sums = functools.reduce(jnp.add, [e * pltpu.roll(x, LANES - 1, 1) for e, x in zip(factors, info)])
    wide = [jnp.broadcast_to(e[:, 0:1], (rows, LANES)) for e in factors]
    inv = 1.0 / sums[:, 0:1]
    for k in range(chunks):
        acc = functools.reduce(jnp.add, [wide[d] * got_ref[per * d + k] for d in range(pairs)])
        readout_ref[:, k * LANES : (k + 1) * LANES] = (acc * inv).astype(BF16)
    logprob_ref[...] = total[:, 4:12] - (top[:, 2:3] + jnp.log(sums[:, 2:3]))


def per_device(queries, centroids, leaves, beam):
    groups = lax.axis_size("cluster")
    rows, width = queries.shape
    count, leaf_count, _ = leaves.shape
    top = beam.shape[1]
    pairs = groups // 2
    half = pairs * rows
    total = 2 * half
    scale = 1.0 / math.sqrt(width)
    me = lax.axis_index("cluster")
    side = me % 2
    sides = [[2 * i + c for i in range(pairs)] for c in range(2)]
    swap = [(i, i ^ 1) for i in range(groups)]
    vmem = pl.BlockSpec(memory_space=pltpu.VMEM)

    hbm = pl.BlockSpec(memory_space=pltpu.HBM)
    leaves, centroids = (pltpu.with_memory_space_constraint(a, pltpu.HBM) for a in (leaves, centroids))

    spread = jnp.broadcast_to(queries[None], (pairs, rows, width))
    own = lax.all_to_all(spread, "cluster", 0, 0, axis_index_groups=sides)
    own, beam = lax.optimization_barrier((own, beam))
    other = lax.ppermute(own, "cluster", swap)
    slots = count * CAP
    tables = pl.pallas_call(
        table_kernel,
        out_shape=(
            jax.ShapeDtypeStruct((slots, total), BF16),
            jax.ShapeDtypeStruct((total, slots), BF16),
            jax.ShapeDtypeStruct((top, total), jnp.int32),
            jax.ShapeDtypeStruct(centroids.shape, BF16),
            jax.ShapeDtypeStruct((AHEAD, leaf_count, width), BF16),
        ),
        in_specs=[hbm] * 3,
        out_specs=(vmem,) * 5,
        scratch_shapes=[pltpu.VMEM((top, total), jnp.int32), pltpu.SemaphoreType.DMA((2 + AHEAD,))],
        compiler_params=pltpu.CompilerParams(vmem_limit_bytes=4 << 20),
        cost_estimate=pl.CostEstimate(flops=50_000_000, bytes_accessed=4 << 20, transcendentals=0),
        name="table",
    )(pltpu.with_memory_space_constraint(beam.T, pltpu.HBM), centroids, leaves)
    state = jax.ShapeDtypeStruct((width // LANES * half + 16, LANES), F32)
    mine, theirs = pl.pallas_call(
        functools.partial(leaf_kernel, scale),
        out_shape=(state, state),
        in_specs=[vmem] * 7 + [hbm],
        out_specs=(vmem, vmem),
        scratch_shapes=[pltpu.VMEM((count - AHEAD, leaf_count, width), BF16), pltpu.SemaphoreType.DMA((count - AHEAD,))],
        compiler_params=pltpu.CompilerParams(vmem_limit_bytes=24 << 20),
        name="leaf",
    )(own.reshape(half, width), other.reshape(half, width), *tables, leaves)
    theirs = lax.ppermute(theirs, "cluster", swap)
    per = width // LANES + 1
    packed = pl.pallas_call(
        merge_kernel,
        out_shape=jax.ShapeDtypeStruct((pairs * per, rows, LANES), F32),
        in_specs=[vmem, vmem],
        out_specs=vmem,
        compiler_params=pltpu.CompilerParams(vmem_limit_bytes=8 << 20),
        name="merge",
    )(mine, theirs)
    got = lax.all_to_all(packed, "cluster", 0, 0, axis_index_groups=sides, tiled=True)
    return pl.pallas_call(
        home_kernel,
        out_shape=(jax.ShapeDtypeStruct((rows, width), BF16), jax.ShapeDtypeStruct((rows, top), F32)),
        in_specs=[vmem],
        out_specs=(vmem, vmem),
        compiler_params=pltpu.CompilerParams(vmem_limit_bytes=8 << 20),
        name="home",
    )(got)


def solution(mesh):
    return jax.shard_map(
        per_device,
        mesh=mesh,
        in_specs=(
            P(("query", "cluster"), None),
            P("cluster", None),
            P("cluster", None, None),
            P("query", None),
        ),
        out_specs=(P(("query", "cluster"), None), P(("query", "cluster"), None)),
        check_vma=False,
    )
```

time: 62.4 us -> 50.1 us (0.80)
  blocking collectives: 0 us -> 39 us
  waiting for transfers between devices: 25.5 us -> 1.18 us
  starting transfers between devices: 15.7 us -> 0.6 us
  matrix products: 11.4 us -> 0 us
  Pallas kernels: 0 us -> 7.68 us
  local copies, waits for them, and re-layouts: 5.7 us -> 0.8 us
  other arithmetic: 2.82 us -> 0 us
    all_to_all x0 -> x2, blocking collectives: none -> 39 us  [the longest x1 20.8 us: per_device(): own = lax.all_to_all(spread, 'cluster', 0, 0, axis_index_groups=sides)]
    all_to_all x2 -> x0, waiting for transfers between devices: 22.7 us -> none  [the longest x1 14.1 us: per_device(): lax.all_to_all(state.reshape(pairs, rows, width + 128), 'cluster', 0, 0,...]
    all_to_all x2 -> x0, starting transfers between devices: 15.5 us -> none  [the longest x1 11.2 us: per_device(): lax.all_to_all(jnp.broadcast_to(queries[None], (pairs, rows, width)), 'cl...]
    dot_general x5 -> x0, matrix products: 11.4 us -> none  [the longest x1 5.86 us: per_device(): jnp.einsum('csd,cjd->csj', picked, leaves, preferred_element_type=jnp.flo...]
    pallas_call x0 -> x4, Pallas kernels: none -> 7.68 us  [the longest x1 5.02 us: per_device(): pl.pallas_call(functools.partial(leaf_kernel, scale), out_shape=(state, s...]
    unnamed x7 -> x0, local copies, waits for them, and re-layouts: 1.84 us -> none
    ppermute x2, waiting for transfers between devices: 2.76 us -> 1.18 us  [the longest x1 1.17 us: per_device(): theirs = lax.ppermute(theirs, 'cluster', swap)]
    reduce_sum x7 -> x0, other arithmetic: 1.28 us -> none  [the longest x1 0.23 us: per_device(): jnp.sum(jnp.exp(scores - cmax[None, :, None]), axis=(0, 2))]
  transfers between devices with their start and end apart: 4 -> 2, of which waited for: 4 -> 1; matrix products, arithmetic and copies ran while one was open for 2% -> 0% of each run, Pallas kernels for 0% -> 3%
where the time goes in v2:
time: 50.1 us; the launch traced here: 49.9 us
  blocking collectives  39 us (78%)
  Pallas kernels  7.68 us (15%)
  waiting for transfers between devices  1.18 us (2%)
  local copies, waits for them, and re-layouts  0.8 us (2%)
  between operations  0.67 us (1%)
  starting transfers between devices  0.6 us (1%)
    all_to_all x1, blocking collectives, per_device(): own = lax.all_to_all(spread, 'cluster', 0, 0, axis_index_groups=sides)  20.8 us
    all_to_all x1, blocking collectives, per_device(): lax.all_to_all(packed, 'cluster', 0, 0, axis_index_groups=sides, tiled=True)  18.2 us
    pallas_call x1, Pallas kernels, per_device(): pl.pallas_call(functools.partial(leaf_kernel, scale), out_shape=(state, s...  5.02 us
    pallas_call x1, Pallas kernels, per_device(): pl.pallas_call(table_kernel, out_shape=(jax.ShapeDtypeStruct((slots, tota...  1.61 us
    ppermute x1, waiting for transfers between devices, per_device(): theirs = lax.ppermute(theirs, 'cluster', swap)  1.17 us
  transfers between devices with their start and end apart: 2, of which 1 were waited for; matrix products, arithmetic and copies ran while one was open for 0% of the time, Pallas kernels for 3%

profile of v2, /device:TPU:32, one launch (start us, length us, event | category | flops | bytes accessed | tf_op | source)
XLA Modules:
  0.0 49.9 jit_solution(9407646074548892007)
XLA Ops:
  0.6 0.7 %broadcast_in_dim.2 = bf16[32,4,512]{2,1,0:T(4,128)(2,1)S(1)} broadcast(bf16[4,512]{1,0:T(4,128)(2,1)} %param.4), dimensions={1,2} | broadcast | bytes 135168 | tf_op jit(solution)/shard_map/broadcast_in_dim | solution.py:188
  1.4 20.8 %all_to_all.10 = bf16[32,4,512]{2,1,0:T(4,128)(2,1)S(1)} all-to-all(bf16[32,4,512]{2,1,0:T(4,128)(2,1)S(1)} %broadcast_in_dim.2), channel_id=1, replica_groups={{0,2,4,6,8,10,12,14,16,18,20,22,24,26,28,30,32,34,36,38,40,42,44,46,48,..., dimensions={0} | all-to-all | bytes 262144 | tf_op jit(solution)/shard_map/all_to_all | solution.py:189
  22.1 0.0 collective-permute-start
  22.2 1.6 %table.1 = (bf16[64,256]{1,0:T(8,128)(2,1)S(1)}, bf16[256,64]{1,0:T(8,128)(2,1)S(1)}, s32[8,256]{1,0:T(8,128)S(1)}, bf16[8,512]{1,0:T(8,128)(2,1)S(1)}, bf16[2,1024,512]{2,1,0:T(8,128)(2,1)S(1)}) custom-call(s32[8,256]{1,0:T(8,128)} %bitcast.1, bf16[8,512]{1,0:T(8,128)(2,1)} %cent_ref.1, bf16[8,1024,512]{2,1,0:T(8,128)(2,1)} %leaves_ref.3), custom_call_target="tpu_custom_call" | custom-call | flops 50000000 | bytes 4194304 | tf_op jit(solution)/shard_map/table/pallas_call | solution.py:193
  23.8 0.0 collective-permute-done
  23.8 5.0 %leaf.1 = (f32[528,128]{1,0:T(8,128)S(1)}, f32[528,128]{1,0:T(8,128)S(1)}) custom-call(bf16[128,512]{1,0:T(8,128)(2,1)S(1)} %reshape.11.own_ref, bf16[128,512]{1,0:T(8,128)(2,1)S(1)} %reshape.12.other_ref, bf16[64,256]{1,0:T(8,128)(2,1)S(1)} %get-tuple-element.13.disp_ref, bf16[256,64]{1,0:T(8,128)(2,1)S(1)} %get-tuple-element.14.disp_t_ref, ...), custom_call_target="tpu_custom_call" | custom-call | tf_op jit(solution)/shard_map/leaf/pallas_call | solution.py:210
  28.9 0.6 %collective-permute-start.1 = (f32[528,128]{1,0:T(8,128)S(1)}, f32[528,128]{1,0:T(8,128)S(1)}, u32[]{:S(2)}, u32[]{:S(2)}) collective-permute-start(f32[528,128]{1,0:T(8,128)S(1)} %get-tuple-element.19), channel_id=1, source_target_pairs={{0,1},{1,0},{2,3},{3,2},{4,5},{5,4},{6,7},{7,6},{8,9},{9,8},{10,11... | collective-permute-start | bytes 811016 | tf_op jit(solution)/shard_map/ppermute | solution.py:219
  29.5 1.2 %collective-permute-done.1.theirs_ref = f32[528,128]{1,0:T(8,128)S(1)} collective-permute-done((f32[528,128]{1,0:T(8,128)S(1)}, f32[528,128]{1,0:T(8,128)S(1)}, u32[]{:S(2)}, u32[]{:S(2)}) %collective-permute-start.1) | collective-permute-done | bytes 270368 | tf_op jit(solution)/shard_map/ppermute | solution.py:219
  30.6 0.2 merge.1
  30.9 18.2 %all_to_all.11.got_ref = f32[160,4,128]{2,1,0:T(4,128)S(1)} all-to-all(f32[160,4,128]{2,1,0:T(4,128)S(1)} %merge.1), channel_id=1, replica_groups={{0,2,4,6,8,10,12,14,16,18,20,22,24,26,28,30,32,34,36,38,40,42,44,46,48,..., dimensions={0} | all-to-all | bytes 655360 | tf_op jit(solution)/shard_map/all_to_all | solution.py:229
  49.1 0.8 %home.1 = (bf16[4,512]{1,0:T(4,128)(2,1)}, f32[4,8]{1,0:T(4,128)}) custom-call(f32[160,4,128]{2,1,0:T(4,128)S(1)} %all_to_all.11.got_ref), custom_call_target="tpu_custom_call" | custom-call | tf_op jit(solution)/shard_map/home/pallas_call | solution.py:230
  (2 shorter events, 0.1 us)
Async XLA Ops:
  22.1 1.7 %collective-permute-start = (bf16[32,4,512]{2,1,0:T(4,128)(2,1)S(1)}, bf16[32,4,512]{2,1,0:T(4,128)(2,1)S(1)}, u32[]{:S(2)}, u32[]{:S(2)}) collective-permute-start(bf16[32,4,512]{2,1,0:T(4,128)(2,1)S(1)} %all_to_all.10), channel_id=1, source_target_pairs={{0,1},{1,0},{2,3},{3,2},{4,5},{5,4},{6,7},{7,6},{8,9},{9,8},{10,11... | collective-permute-start | bytes 393224 | tf_op jit(solution)/shard_map/ppermute | solution.py:191
  28.9 1.8 %collective-permute-start.1 = (f32[528,128]{1,0:T(8,128)S(1)}, f32[528,128]{1,0:T(8,128)S(1)}, u32[]{:S(2)}, u32[]{:S(2)}) collective-permute-start(f32[528,128]{1,0:T(8,128)S(1)} %get-tuple-element.19), channel_id=1, source_target_pairs={{0,1},{1,0},{2,3},{3,2},{4,5},{5,4},{6,7},{7,6},{8,9},{9,8},{10,11... | collective-permute-start | bytes 811016 | tf_op jit(solution)/shard_map/ppermute | solution.py:219

commit v3 on v2

--- a/solution.py
+++ b/solution.py
@@ -8,7 +8,7 @@
 from jax.experimental.pallas import tpu as pltpu
 from jax.sharding import PartitionSpec as P
 
-FLOOR = -1e30
+FLOOR = -30000.0
 CAP = 8
 AHEAD = 2
 LANES = 128
@@ -55,7 +55,7 @@
         [jnp.where(slot == rank[c : c + 1], 1.0, 0.0) * hits[c] for c in range(count)], axis=0
     ).astype(BF16)
     disp_ref[...] = dot(disp, order, 1, 1).astype(BF16)
-    disp_t_ref[...] = dot(order, disp, 1, 1).astype(BF16)
+    disp_t_ref[...] = dot(order, jnp.concatenate([disp, disp], axis=0), 1, 1).astype(BF16)
     coarse = beam // 16 * 16
     halves = jnp.concatenate([coarse, beam - coarse], axis=0).astype(F32).astype(BF16)
     halves = dot(halves, order, 1, 1)
@@ -118,8 +118,7 @@
     f = jnp.exp(jnp.minimum(m - back, 0.0))
     q_l = jnp.sum(jnp.where(on, f * l, 0.0), axis=0, keepdims=True)
     hi, lo = pieces(f * acc)
-    disp_t = disp_t_ref[...]
-    q_acc = dot(disp_t, hi, 1, 0) + dot(disp_t, lo, 1, 0)
+    q_acc = dot(disp_t_ref[...], jnp.concatenate([hi, lo], axis=0), 1, 0)
     rows = jnp.concatenate([q_m, q_l, c_m, c_l, score, jnp.zeros((4, total), F32)], axis=0)
     for side, ref in enumerate((mine_ref, theirs_ref)):
         for k in range(width // LANES):
@@ -137,14 +136,26 @@
     l = fa * a[1:2] + fb * b[1:2]
     c = jnp.maximum(a[2:3], b[2:3])
     cl = jnp.exp(a[2:3] - c) * a[3:4] + jnp.exp(b[2:3] - c) * b[3:4]
-    block = jnp.concatenate([m, l, c, cl, a[4:12] + b[4:12], fa, fb, jnp.zeros((LANES - 14, half), F32)], axis=0)
+    inv = 1.0 / jnp.maximum(l, 1e-30)
+    info = jnp.concatenate([m, l, c, cl, a[4:12] + b[4:12], jnp.zeros((4, half), F32)], axis=0)
+    hi = info.astype(BF16).astype(F32)
+    rest = info - hi
+    mid = rest.astype(BF16).astype(F32)
+    block = jnp.concatenate(
+        [hi, mid * 256.0, (rest - mid) * 65536.0, fa * inv, fb * inv, jnp.zeros((LANES - 50, half), F32)], axis=0
+    )
     cols = block.T
-    fa, fb = cols[:, 12:13], cols[:, 13:14]
-    per = out_ref.shape[0] * 4 // half
+    fa, fb = cols[:, 48:49], cols[:, 49:50]
     outs = [
         fa * mine_ref[k * half : (k + 1) * half] + fb * theirs_ref[k * half : (k + 1) * half] for k in range(chunks)
-    ] + [cols]
-    for k, value in enumerate(outs):
+    ]
+    high = jnp.max(functools.reduce(jnp.maximum, [jnp.abs(o) for o in outs]), axis=1, keepdims=True)
+    power = jnp.floor(jnp.log2(jnp.maximum(high, 1e-30)))
+    down = jnp.exp2(-power)
+    lane = lax.broadcasted_iota(jnp.int32, (half, LANES), 1)
+    cols = jnp.where(lane == 12, power, jnp.where(lane < 48, cols, 0.0))
+    per = chunks + 1
+    for k, value in enumerate([o * down for o in outs] + [cols]):
         for d in range(half // 4):
             out_ref[per * d + k] = value[4 * d : 4 * d + 4]
 
@@ -154,17 +165,31 @@
     chunks = width // LANES
     per = chunks + 1
     pairs = got_ref.shape[0] // per
-    info = [got_ref[per * d + chunks] for d in range(pairs)]
-    top = functools.reduce(jnp.maximum, info)
-    total = functools.reduce(jnp.add, info)
-    factors = [jnp.exp(x - top) for x in info]
-    sums = functools.reduce(jnp.add, [e * pltpu.roll(x, LANES - 1, 1) for e, x in zip(factors, info)])
-    wide = [jnp.broadcast_to(e[:, 0:1], (rows, LANES)) for e in factors]
-    inv = 1.0 / sums[:, 0:1]
+    info = jnp.concatenate([got_ref[per * d + chunks] for d in range(pairs)], axis=0)
+
+    def left(x, n):
+        return pltpu.roll(x, LANES - n, 1)
+
+    info = info + left(info, 16) * (1.0 / 256.0) + left(info, 32) * (1.0 / 65536.0)
+    tiles = [info[8 * t : 8 * t + 8] for t in range(pairs * rows // 8)]
+
+    def fold(op, xs):
+        x = functools.reduce(op, xs)
+        return op(x, pltpu.roll(x, 4, 0))
+
+    top = fold(jnp.maximum, tiles)
+    total = fold(jnp.add, tiles)
+    prods = [jnp.exp(x - top) * left(x, 1) for x in tiles]
+    sums = fold(jnp.add, prods)
+    coefs = [
+        jnp.broadcast_to(p[:, 0:1] * jnp.exp2(x[:, 12:13]), (8, LANES)) for p, x in zip(prods, tiles)
+    ]
+    coefs = [coefs[d // 2][d % 2 * 4 : d % 2 * 4 + 4] for d in range(pairs)]
+    inv = 1.0 / sums[:rows, 0:1]
     for k in range(chunks):
-        acc = functools.reduce(jnp.add, [wide[d] * got_ref[per * d + k] for d in range(pairs)])
+        acc = functools.reduce(jnp.add, [coefs[d] * got_ref[per * d + k] for d in range(pairs)])
         readout_ref[:, k * LANES : (k + 1) * LANES] = (acc * inv).astype(BF16)
-    logprob_ref[...] = total[:, 4:12] - (top[:, 2:3] + jnp.log(sums[:, 2:3]))
+    logprob_ref[...] = total[:rows, 4:12] - (top[:rows, 2:3] + jnp.log(sums[:rows, 2:3]))
 
 
 def per_device(queries, centroids, leaves, beam):
@@ -194,7 +219,7 @@
         table_kernel,
         out_shape=(
             jax.ShapeDtypeStruct((slots, total), BF16),
-            jax.ShapeDtypeStruct((total, slots), BF16),
+            jax.ShapeDtypeStruct((total, 2 * slots), BF16),
             jax.ShapeDtypeStruct((top, total), jnp.int32),
             jax.ShapeDtypeStruct(centroids.shape, BF16),
             jax.ShapeDtypeStruct((AHEAD, leaf_count, width), BF16),
@@ -226,7 +251,8 @@
         compiler_params=pltpu.CompilerParams(vmem_limit_bytes=8 << 20),
         name="merge",
     )(mine, theirs)
-    got = lax.all_to_all(packed, "cluster", 0, 0, axis_index_groups=sides, tiled=True)
+    packed = packed.astype(jnp.float16)
+    got = lax.all_to_all(packed, "cluster", 0, 0, axis_index_groups=sides, tiled=True).astype(F32)
     return pl.pallas_call(
         home_kernel,
         out_shape=(jax.ShapeDtypeStruct((rows, width), BF16), jax.ShapeDtypeStruct((rows, top), F32)),

time: 50.1 us -> 47.7 us (0.952); the launches traced: 49.9 us -> 46.9 us
  blocking collectives: 39 us -> 35.8 us
    all_to_all x1, blocking collectives: 18.2 us -> 15 us  [per_device(): lax.all_to_all(packed, 'cluster', 0, 0, axis_index_groups=sides, tiled=True)]
where the time goes in v3:
time: 47.7 us; the launch traced here: 46.9 us
  blocking collectives  35.8 us (75%)
  Pallas kernels  7.72 us (16%)
  waiting for transfers between devices  1.18 us (2%)
  local copies, waits for them, and re-layouts  0.8 us (2%)
  between operations  0.68 us (1%)
  starting transfers between devices  0.6 us (1%)
    all_to_all x1, blocking collectives, per_device(): own = lax.all_to_all(spread, 'cluster', 0, 0, axis_index_groups=sides)  20.8 us
    all_to_all x1, blocking collectives, per_device(): lax.all_to_all(packed, 'cluster', 0, 0, axis_index_groups=sides, tiled=True)  15 us
    pallas_call x1, Pallas kernels, per_device(): pl.pallas_call(functools.partial(leaf_kernel, scale), out_shape=(state, s...  4.89 us
    pallas_call x1, Pallas kernels, per_device(): pl.pallas_call(table_kernel, out_shape=(jax.ShapeDtypeStruct((slots, tota...  1.61 us
    ppermute x1, waiting for transfers between devices, per_device(): theirs = lax.ppermute(theirs, 'cluster', swap)  1.17 us
  transfers between devices with their start and end apart: 2, of which 1 were waited for; matrix products, arithmetic and copies ran while one was open for 0% of the time, Pallas kernels for 3%

profile of v3, /device:TPU:32, one launch (start us, length us, event | category | flops | bytes accessed | tf_op | source)
XLA Modules:
  0.0 46.9 jit_solution(12957889787970088871)
XLA Ops:
  0.6 0.7 %broadcast_in_dim.2 = bf16[32,4,512]{2,1,0:T(4,128)(2,1)S(1)} broadcast(bf16[4,512]{1,0:T(4,128)(2,1)} %param.4), dimensions={1,2} | broadcast | bytes 135168 | tf_op jit(solution)/shard_map/broadcast_in_dim | solution.py:213
  1.4 20.8 %all_to_all.10 = bf16[32,4,512]{2,1,0:T(4,128)(2,1)S(1)} all-to-all(bf16[32,4,512]{2,1,0:T(4,128)(2,1)S(1)} %broadcast_in_dim.2), channel_id=1, replica_groups={{0,2,4,6,8,10,12,14,16,18,20,22,24,26,28,30,32,34,36,38,40,42,44,46,48,..., dimensions={0} | all-to-all | bytes 262144 | tf_op jit(solution)/shard_map/all_to_all | solution.py:214
  22.1 0.0 collective-permute-start
  22.2 1.6 %table.1 = (bf16[64,256]{1,0:T(8,128)(2,1)S(1)}, bf16[256,128]{1,0:T(8,128)(2,1)S(1)}, s32[8,256]{1,0:T(8,128)S(1)}, bf16[8,512]{1,0:T(8,128)(2,1)S(1)}, bf16[2,1024,512]{2,1,0:T(8,128)(2,1)S(1)}) custom-call(s32[8,256]{1,0:T(8,128)} %bitcast.1, bf16[8,512]{1,0:T(8,128)(2,1)} %cent_ref.1, bf16[8,1024,512]{2,1,0:T(8,128)(2,1)} %leaves_ref.3), custom_call_target="tpu_custom_call" | custom-call | flops 50000000 | bytes 4194304 | tf_op jit(solution)/shard_map/table/pallas_call | solution.py:218
  23.8 0.0 collective-permute-done
  23.8 4.9 %leaf.1 = (f32[528,128]{1,0:T(8,128)S(1)}, f32[528,128]{1,0:T(8,128)S(1)}) custom-call(bf16[128,512]{1,0:T(8,128)(2,1)S(1)} %reshape.11.own_ref, bf16[128,512]{1,0:T(8,128)(2,1)S(1)} %reshape.12.other_ref, bf16[64,256]{1,0:T(8,128)(2,1)S(1)} %get-tuple-element.13.disp_ref, bf16[256,128]{1,0:T(8,128)(2,1)S(1)} %get-tuple-element.14.disp_t_ref, ...), custom_call_target="tpu_custom_call" | custom-call | tf_op jit(solution)/shard_map/leaf/pallas_call | solution.py:235
  28.7 0.6 %collective-permute-start.1 = (f32[528,128]{1,0:T(8,128)S(1)}, f32[528,128]{1,0:T(8,128)S(1)}, u32[]{:S(2)}, u32[]{:S(2)}) collective-permute-start(f32[528,128]{1,0:T(8,128)S(1)} %get-tuple-element.19), channel_id=1, source_target_pairs={{0,1},{1,0},{2,3},{3,2},{4,5},{5,4},{6,7},{7,6},{8,9},{9,8},{10,11... | collective-permute-start | bytes 811016 | tf_op jit(solution)/shard_map/ppermute | solution.py:244
  29.3 1.2 %collective-permute-done.1.theirs_ref = f32[528,128]{1,0:T(8,128)S(1)} collective-permute-done((f32[528,128]{1,0:T(8,128)S(1)}, f32[528,128]{1,0:T(8,128)S(1)}, u32[]{:S(2)}, u32[]{:S(2)}) %collective-permute-start.1) | collective-permute-done | bytes 270368 | tf_op jit(solution)/shard_map/ppermute | solution.py:244
  30.5 0.3 merge.1
  30.8 0.1 convert_element_type.6
  30.9 15.0 %all_to_all.11 = f16[160,4,128]{2,1,0:T(4,128)(2,1)S(1)} all-to-all(f16[160,4,128]{2,1,0:T(4,128)(2,1)S(1)} %convert_element_type.6), channel_id=1, replica_groups={{0,2,4,6,8,10,12,14,16,18,20,22,24,26,28,30,32,34,36,38,40,42,44,46,48,..., dimensions={0} | all-to-all | bytes 327680 | tf_op jit(solution)/shard_map/all_to_all | solution.py:255
  45.9 0.1 convert_element_type.7.got_ref
  46.0 0.9 %home.1 = (bf16[4,512]{1,0:T(4,128)(2,1)}, f32[4,8]{1,0:T(4,128)}) custom-call(f32[160,4,128]{2,1,0:T(4,128)S(1)} %convert_element_type.7.got_ref), custom_call_target="tpu_custom_call" | custom-call | tf_op jit(solution)/shard_map/home/pallas_call | solution.py:256
  (2 shorter events, 0.1 us)
Async XLA Ops:
  22.1 1.7 %collective-permute-start = (bf16[32,4,512]{2,1,0:T(4,128)(2,1)S(1)}, bf16[32,4,512]{2,1,0:T(4,128)(2,1)S(1)}, u32[]{:S(2)}, u32[]{:S(2)}) collective-permute-start(bf16[32,4,512]{2,1,0:T(4,128)(2,1)S(1)} %all_to_all.10), channel_id=1, source_target_pairs={{0,1},{1,0},{2,3},{3,2},{4,5},{5,4},{6,7},{7,6},{8,9},{9,8},{10,11... | collective-permute-start | bytes 393224 | tf_op jit(solution)/shard_map/ppermute | solution.py:216
  28.7 1.8 %collective-permute-start.1 = (f32[528,128]{1,0:T(8,128)S(1)}, f32[528,128]{1,0:T(8,128)S(1)}, u32[]{:S(2)}, u32[]{:S(2)}) collective-permute-start(f32[528,128]{1,0:T(8,128)S(1)} %get-tuple-element.19), channel_id=1, source_target_pairs={{0,1},{1,0},{2,3},{3,2},{4,5},{5,4},{6,7},{7,6},{8,9},{9,8},{10,11... | collective-permute-start | bytes 811016 | tf_op jit(solution)/shard_map/ppermute | solution.py:244

commit v4 on v3

v4 whole, which is shorter than its diff:
```python
import functools
import math

import jax
import jax.numpy as jnp
from jax import lax
from jax.experimental import pallas as pl
from jax.experimental.pallas import tpu as pltpu
from jax.sharding import PartitionSpec as P

FLOOR = -30000.0
CAP = 8
LANES = 128
F32 = jnp.float32
BF16 = jnp.bfloat16


def dot(a, b, ca, cb):
    return lax.dot_general(a, b, (((ca,), (cb,)), ((), ())), preferred_element_type=F32)


def pieces(x):
    hi = x.astype(BF16)
    lo = (x - hi.astype(F32)).astype(BF16)
    return hi, lo


def table_kernel(beam_ref, cent_ref, disp_ref, mine_ref, mine_t_ref, turned_ref, cent_out, beam_buf, sems):
    count = cent_ref.shape[0]
    total = beam_ref.shape[1]
    half = total // 2
    rows = total // lax.axis_size("cluster")
    copies = [
        pltpu.make_async_copy(beam_ref, beam_buf, sems.at[0]),
        pltpu.make_async_copy(cent_ref, cent_out, sems.at[1]),
    ]
    for copy in copies:
        copy.start()
    me = lax.axis_index("cluster")
    square = (total, total)
    down, across = (lax.broadcasted_iota(jnp.int32, square, d) for d in range(2))
    upper = jnp.where(down <= across, 1.0, 0.0).astype(BF16)
    r = lax.broadcasted_iota(jnp.int32, (total, 1), 0)
    p, r = r // half, r % half
    source = (r // rows * 2 + (p + me) % 2) * rows + r % rows
    order = jnp.where(source == across, 1.0, 0.0).astype(BF16)
    copies[0].wait()
    beam = beam_buf[...]
    firsts = ((me + 1 - 2 * (me % 2)) * count, me * count)
    hits = [
        jnp.max(jnp.where(beam == first + c, 1.0, 0.0), axis=0, keepdims=True) for first in firsts for c in range(count)
    ]
    rank = dot(jnp.concatenate(hits, axis=0).astype(BF16), upper, 1, 0)
    slot = lax.broadcasted_iota(jnp.int32, (CAP, total), 0).astype(F32) + 1.0
    disp = jnp.concatenate(
        [jnp.where(slot == rank[c : c + 1], 1.0, 0.0) * hits[c] for c in range(2 * count)], axis=0
    ).astype(BF16)
    turned = dot(disp, order, 1, 1).astype(BF16)
    disp_ref[...] = turned[: count * CAP]
    mine_ref[...] = turned[:, :half]
    mine_t_ref[...] = dot(order[:half], jnp.concatenate([disp, disp], axis=0), 1, 1).astype(BF16)
    coarse = beam // 16 * 16
    halves = jnp.concatenate([coarse, beam - coarse], axis=0).astype(F32).astype(BF16)
    halves = dot(halves, order[:half], 1, 1)
    top = beam.shape[0]
    turned_ref[...] = (halves[:top] + halves[top:]).astype(jnp.int32)
    copies[1].wait()


def leaf_kernel(scale, own_ref, other_ref, disp_ref, cent_ref, leaves_ref, pack_ref, info_ref, q_ref):
    count, leaf_count, width = leaves_ref.shape
    pairs, rows, _ = own_ref.shape
    half = pairs * rows
    total = 2 * half
    for side, ref in enumerate((own_ref, other_ref)):
        for d in range(pairs):
            q_ref[side * half + d * rows : side * half + (d + 1) * rows] = ref[d]
    q = q_ref[...]
    disp = disp_ref[...]
    picked = dot(disp, q, 1, 0).astype(BF16)
    cs = dot(cent_ref[...], q, 1, 1) * scale
    def scores(c):
        return dot(picked[c * CAP : (c + 1) * CAP], leaves_ref[c], 1, 1)

    ms, ls, accs = [], [], []
    s = scores(0)
    for c in range(count):
        z = s * scale
        if c + 1 < count:
            s = scores(c + 1)
        m = jnp.max(z, axis=1, keepdims=True)
        w = jnp.exp(z - m)
        ms.append(m)
        ls.append(jnp.sum(w, axis=1, keepdims=True))
        accs.append(dot(w.astype(BF16), leaves_ref[c], 1, 0))
    info_ref[...] = cs[:, :half]
    slots = count * CAP
    for c in range(count):
        for k in range(width // LANES):
            pack_ref[k * slots + c * CAP : k * slots + (c + 1) * CAP] = accs[c][:, k * LANES : (k + 1) * LANES]
    lane = lax.broadcasted_iota(jnp.int32, (slots, LANES), 1)
    base = width // LANES * slots
    pack_ref[base : base + slots] = jnp.where(
        lane == 0, jnp.concatenate(ms, axis=0), jnp.concatenate(ls, axis=0)
    )
    pack_ref[base + slots :] = cs[:, half:]


def merge_kernel(pack_ref, info_ref, theirs_ref, mine_ref, mine_t_ref, beam_ref, out_ref):
    half = info_ref.shape[1]
    slots = mine_ref.shape[0] // 2
    count = info_ref.shape[0]
    chunks = (pack_ref.shape[0] - count) // slots - 1
    base = chunks * slots

    def both(k):
        return jnp.concatenate([ref[k * slots : (k + 1) * slots] for ref in (pack_ref, theirs_ref)], axis=0)

    stats = both(chunks)
    cs = jnp.concatenate([theirs_ref[base + slots :], info_ref[...]], axis=0)
    wide = jnp.concatenate([jnp.broadcast_to(cs[c : c + 1], (CAP, half)) for c in range(2 * count)], axis=0)
    on = mine_ref[...].astype(F32) > 0.5
    slot_m = stats[:, 0:1] + jnp.sum(jnp.where(on, wide, 0.0), axis=1, keepdims=True)
    slot_l = stats[:, 1:2]
    m = jnp.max(jnp.where(on, slot_m, FLOOR), axis=0, keepdims=True)
    back = jnp.sum(jnp.where(on, m, 0.0), axis=1, keepdims=True)
    f = jnp.exp(jnp.minimum(slot_m - back, 0.0))
    l = jnp.sum(jnp.where(on, f * slot_l, 0.0), axis=0, keepdims=True)
    mine_t = mine_t_ref[...]
    accs = []
    for k in range(chunks):
        hi, lo = pieces(f * both(k))
        accs.append(dot(mine_t, jnp.concatenate([hi, lo], axis=0), 1, 0))
    c = jnp.max(cs, axis=0, keepdims=True)
    cl = jnp.sum(jnp.exp(cs - c), axis=0, keepdims=True)
    me = lax.axis_index("cluster")
    firsts = ((me + 1 - 2 * (me % 2)) * count, me * count)
    beam = beam_ref[...]
    score = jnp.zeros(beam.shape, F32)
    for i in range(2 * count):
        score = score + jnp.where(beam == firsts[i // count] + i % count, cs[i : i + 1], 0.0)
    inv = 1.0 / jnp.maximum(l, 1e-30)
    info = jnp.concatenate([m, l, c, cl, score, jnp.zeros((4, half), F32)], axis=0)
    hi = info.astype(BF16).astype(F32)
    rest = info - hi
    mid = rest.astype(BF16).astype(F32)
    block = jnp.concatenate(
        [hi, mid * 256.0, (rest - mid) * 65536.0, inv, jnp.zeros((LANES - 49, half), F32)], axis=0
    )
    cols = block.T
    inv = cols[:, 48:49]
    outs = [acc * inv for acc in accs]
    high = jnp.max(functools.reduce(jnp.maximum, [jnp.abs(o) for o in outs]), axis=1, keepdims=True)
    power = jnp.floor(jnp.log2(jnp.maximum(high, 1e-30)))
    down = jnp.exp2(-power)
    lane = lax.broadcasted_iota(jnp.int32, (half, LANES), 1)
    cols = jnp.where(lane == 12, power, jnp.where(lane < 48, cols, 0.0))
    per = chunks + 1
    for k, value in enumerate([o * down for o in outs] + [cols]):
        for d in range(half // 4):
            out_ref[per * d + k] = value[4 * d : 4 * d + 4]


def home_kernel(got_ref, readout_ref, logprob_ref):
    rows, width = readout_ref.shape
    chunks = width // LANES
    per = chunks + 1
    pairs = got_ref.shape[0] // per
    info = jnp.concatenate([got_ref[per * d + chunks] for d in range(pairs)], axis=0)

    def left(x, n):
        return pltpu.roll(x, LANES - n, 1)

    info = info + left(info, 16) * (1.0 / 256.0) + left(info, 32) * (1.0 / 65536.0)
    tiles = [info[8 * t : 8 * t + 8] for t in range(pairs * rows // 8)]

    def fold(op, xs):
        x = functools.reduce(op, xs)
        return op(x, pltpu.roll(x, 4, 0))

    top = fold(jnp.maximum, tiles)
    total = fold(jnp.add, tiles)
    prods = [jnp.exp(x - top) * left(x, 1) for x in tiles]
    sums = fold(jnp.add, prods)
    coefs = [
        jnp.broadcast_to(p[:, 0:1] * jnp.exp2(x[:, 12:13]), (8, LANES)) for p, x in zip(prods, tiles)
    ]
    coefs = [coefs[d // 2][d % 2 * 4 : d % 2 * 4 + 4] for d in range(pairs)]
    inv = 1.0 / sums[:rows, 0:1]
    for k in range(chunks):
        acc = functools.reduce(jnp.add, [coefs[d] * got_ref[per * d + k] for d in range(pairs)])
        readout_ref[:, k * LANES : (k + 1) * LANES] = (acc * inv).astype(BF16)
    logprob_ref[...] = total[:rows, 4:12] - (top[:rows, 2:3] + jnp.log(sums[:rows, 2:3]))


def per_device(queries, centroids, leaves, beam):
    groups = lax.axis_size("cluster")
    rows, width = queries.shape
    count, leaf_count, _ = leaves.shape
    top = beam.shape[1]
    pairs = groups // 2
    half = pairs * rows
    total = 2 * half
    scale = 1.0 / math.sqrt(width)
    me = lax.axis_index("cluster")
    side = me % 2
    sides = [[2 * i + c for i in range(pairs)] for c in range(2)]
    swap = [(i, i ^ 1) for i in range(groups)]
    vmem = pl.BlockSpec(memory_space=pltpu.VMEM)

    hbm = pl.BlockSpec(memory_space=pltpu.HBM)
    leaves = lax.ppermute(leaves, "cluster", swap)

    spread = jnp.broadcast_to(queries[None], (pairs, rows, width))
    own = lax.all_to_all(spread, "cluster", 0, 0, axis_index_groups=sides)
    own, beam = lax.optimization_barrier((own, beam))
    other = lax.ppermute(own, "cluster", swap)
    slots = count * CAP
    disp, mine, mine_t, turned, centroids = pl.pallas_call(
        table_kernel,
        out_shape=(
            jax.ShapeDtypeStruct((slots, total), BF16),
            jax.ShapeDtypeStruct((2 * slots, half), BF16),
            jax.ShapeDtypeStruct((half, 4 * slots), BF16),
            jax.ShapeDtypeStruct((top, half), jnp.int32),
            jax.ShapeDtypeStruct(centroids.shape, BF16),
        ),
        in_specs=[hbm] * 2,
        out_specs=(vmem,) * 5,
        scratch_shapes=[pltpu.VMEM((top, total), jnp.int32), pltpu.SemaphoreType.DMA((2,))],
        compiler_params=pltpu.CompilerParams(vmem_limit_bytes=4 << 20),
        cost_estimate=pl.CostEstimate(flops=50_000_000, bytes_accessed=4 << 20, transcendentals=0),
        name="table",
    )(*(pltpu.with_memory_space_constraint(a, pltpu.HBM) for a in (beam.T, centroids)))
    pack, info = pl.pallas_call(
        functools.partial(leaf_kernel, scale),
        out_shape=(
            jax.ShapeDtypeStruct(((width // LANES + 1) * slots + count, LANES), F32),
            jax.ShapeDtypeStruct((count, half), F32),
        ),
        in_specs=[vmem] * 5,
        out_specs=(vmem, vmem),
        scratch_shapes=[pltpu.VMEM((total, width), BF16)],
        compiler_params=pltpu.CompilerParams(vmem_limit_bytes=24 << 20),
        name="leaf",
    )(own, other, disp, centroids, leaves)
    theirs = lax.ppermute(pack, "cluster", swap)
    per = width // LANES + 1
    packed = pl.pallas_call(
        merge_kernel,
        out_shape=jax.ShapeDtypeStruct((pairs * per, rows, LANES), F32),
        in_specs=[vmem] * 6,
        out_specs=vmem,
        compiler_params=pltpu.CompilerParams(vmem_limit_bytes=8 << 20),
        name="merge",
    )(pack, info, theirs, mine, mine_t, turned)
    packed = packed.astype(jnp.float16)
    got = lax.all_to_all(packed, "cluster", 0, 0, axis_index_groups=sides, tiled=True).astype(F32)
    return pl.pallas_call(
        home_kernel,
        out_shape=(jax.ShapeDtypeStruct((rows, width), BF16), jax.ShapeDtypeStruct((rows, top), F32)),
        in_specs=[vmem],
        out_specs=(vmem, vmem),
        compiler_params=pltpu.CompilerParams(vmem_limit_bytes=8 << 20),
        name="home",
    )(got)


def solution(mesh):
    return jax.shard_map(
        per_device,
        mesh=mesh,
        in_specs=(
            P(("query", "cluster"), None),
            P("cluster", None),
            P("cluster", None, None),
            P("query", None),
        ),
        out_specs=(P(("query", "cluster"), None), P(("query", "cluster"), None)),
        check_vma=False,
    )
```

time: 47.7 us -> 46.8 us (0.981)
  Pallas kernels: 7.72 us -> 6.38 us
  blocking collectives: 35.8 us -> 36.4 us
    pallas_call x1, Pallas kernels: 4.89 us -> 3.62 us  [per_device(): pl.pallas_call(functools.partial(leaf_kernel, scale), out_shape=(jax.Shap...]
    all_to_all x1, blocking collectives: 20.8 us -> 21.4 us  [per_device(): own = lax.all_to_all(spread, 'cluster', 0, 0, axis_index_groups=sides)]
    pallas_call x1, Pallas kernels: 1.61 us -> 1.11 us  [per_device(): pl.pallas_call(table_kernel, out_shape=(jax.ShapeDtypeStruct((slots, tota...]
    ppermute x1 -> x2, waiting for transfers between devices: 1.17 us -> 1.1 us  [the longest x1 1.1 us: per_device(): theirs = lax.ppermute(pack, 'cluster', swap)]
  transfers between devices with their start and end apart: 2 -> 3, of which waited for: 1 -> 2; matrix products, arithmetic and copies ran while one was open for 0% -> 2% of each run, Pallas kernels for 3% -> 2%
where the time goes in v4:
time: 46.8 us; the launch traced here: 46 us
  blocking collectives  36.4 us (78%)
  Pallas kernels  6.38 us (14%)
  waiting for transfers between devices  1.32 us (3%)
  local copies, waits for them, and re-layouts  0.72 us (2%)
  between operations  0.67 us (1%)
    all_to_all x1, blocking collectives, per_device(): own = lax.all_to_all(spread, 'cluster', 0, 0, axis_index_groups=sides)  21.4 us
    all_to_all x1, blocking collectives, per_device(): lax.all_to_all(packed, 'cluster', 0, 0, axis_index_groups=sides, tiled=True)  15 us
    pallas_call x1, Pallas kernels, per_device(): pl.pallas_call(functools.partial(leaf_kernel, scale), out_shape=(jax.Shap...  3.62 us
    pallas_call x1, Pallas kernels, per_device(): pl.pallas_call(table_kernel, out_shape=(jax.ShapeDtypeStruct((slots, tota...  1.11 us
    ppermute x1, waiting for transfers between devices, per_device(): theirs = lax.ppermute(pack, 'cluster', swap)  1.1 us
  transfers between devices with their start and end apart: 3, of which 2 were waited for; matrix products, arithmetic and copies ran while one was open for 2% of the time, Pallas kernels for 2%

profile of v4, /device:TPU:32, one launch (start us, length us, event | category | flops | bytes accessed | tf_op | source)
XLA Modules:
  0.0 46.0 jit_solution(17221604414560951355)
XLA Ops:
  0.6 0.1 collective-permute-start.1
  0.7 0.7 %broadcast_in_dim.2 = bf16[32,4,512]{2,1,0:T(4,128)(2,1)S(1)} broadcast(bf16[4,512]{1,0:T(4,128)(2,1)} %param.4), dimensions={1,2} | broadcast | bytes 135168 | tf_op jit(solution)/shard_map/broadcast_in_dim | solution.py:214
  1.5 21.4 %all_to_all.10.own_ref = bf16[32,4,512]{2,1,0:T(4,128)(2,1)S(1)} all-to-all(bf16[32,4,512]{2,1,0:T(4,128)(2,1)S(1)} %broadcast_in_dim.2), channel_id=1, replica_groups={{0,2,4,6,8,10,12,14,16,18,20,22,24,26,28,30,32,34,36,38,40,42,44,46,48,..., dimensions={0} | all-to-all | bytes 262144 | tf_op jit(solution)/shard_map/all_to_all | solution.py:215
  22.9 0.0 collective-permute-start
  22.9 1.1 %table.1 = (bf16[64,256]{1,0:T(8,128)(2,1)S(1)}, bf16[128,128]{1,0:T(8,128)(2,1)S(1)}, bf16[128,256]{1,0:T(8,128)(2,1)S(1)}, s32[8,128]{1,0:T(8,128)S(1)}, bf16[8,512]{1,0:T(8,128)(2,1)S(1)}) custom-call(s32[8,256]{1,0:T(8,128)} %bitcast.1, bf16[8,512]{1,0:T(8,128)(2,1)} %cent_ref.1), custom_call_target="tpu_custom_call" | custom-call | flops 50000000 | bytes 4194304 | tf_op jit(solution)/shard_map/table/pallas_call | solution.py:219
  24.0 0.2 collective-permute-done.other_ref
  24.2 0.0 collective-permute-done.1.leaves_ref
  24.2 3.6 %leaf.1 = (f32[328,128]{1,0:T(8,128)S(1)}, f32[8,128]{1,0:T(8,128)S(1)}) custom-call(bf16[32,4,512]{2,1,0:T(4,128)(2,1)S(1)} %all_to_all.10.own_ref, bf16[32,4,512]{2,1,0:T(4,128)(2,1)S(1)} %collective-permute-done.other_ref, bf16[64,256]{1,0:T(8,128)(2,1)S(1)} %get-tuple-element.13.disp_ref, bf16[8,512]{1,0:T(8,128)(2,1)S(1)} %get-tuple-element.14.cent_ref, ...), custom_call_target="tpu_custom_call" | custom-call | tf_op jit(solution)/shard_map/leaf/pallas_call | solution.py:235
  27.8 0.3 collective-permute-start.2
  28.1 1.1 %collective-permute-done.2.theirs_ref = f32[328,128]{1,0:T(8,128)S(1)} collective-permute-done((f32[328,128]{1,0:T(8,128)S(1)}, f32[328,128]{1,0:T(8,128)S(1)}, u32[]{:S(2)}, u32[]{:S(2)}) %collective-permute-start.2) | collective-permute-done | bytes 167968 | tf_op jit(solution)/shard_map/ppermute | solution.py:247
  29.2 0.7 %merge.1 = f32[160,4,128]{2,1,0:T(4,128)S(1)} custom-call(f32[328,128]{1,0:T(8,128)S(1)} %get-tuple-element.15.pack_ref, f32[8,128]{1,0:T(8,128)S(1)} %get-tuple-element.16.info_ref, f32[328,128]{1,0:T(8,128)S(1)} %collective-permute-done.2.theirs_ref, bf16[128,128]{1,0:T(8,128)(2,1)S(1)} %get-tuple-element.17.mine_ref, ...), custom_call_target="tpu_custom_call" | custom-call | tf_op jit(solution)/shard_map/merge/pallas_call | solution.py:249
  30.0 0.1 convert_element_type.6
  30.1 15.0 %all_to_all.11 = f16[160,4,128]{2,1,0:T(4,128)(2,1)S(1)} all-to-all(f16[160,4,128]{2,1,0:T(4,128)(2,1)S(1)} %convert_element_type.6), channel_id=1, replica_groups={{0,2,4,6,8,10,12,14,16,18,20,22,24,26,28,30,32,34,36,38,40,42,44,46,48,..., dimensions={0} | all-to-all | bytes 327680 | tf_op jit(solution)/shard_map/all_to_all | solution.py:258
  45.0 0.1 convert_element_type.7.got_ref
  45.1 0.9 %home.1 = (bf16[4,512]{1,0:T(4,128)(2,1)}, f32[4,8]{1,0:T(4,128)}) custom-call(f32[160,4,128]{2,1,0:T(4,128)S(1)} %convert_element_type.7.got_ref), custom_call_target="tpu_custom_call" | custom-call | tf_op jit(solution)/shard_map/home/pallas_call | solution.py:259
Async XLA Ops:
  0.6 23.6 %collective-permute-start.1 = (bf16[8,1024,512]{2,1,0:T(8,128)(2,1)}, bf16[8,1024,512]{2,1,0:T(8,128)(2,1)S(1)}, u32[]{:S(2)}, u32[]{:S(2)}) collective-permute-start(bf16[8,1024,512]{2,1,0:T(8,128)(2,1)} %param.6), channel_id=1, source_target_pairs={{0,1},{1,0},{2,3},{3,2},{4,5},{5,4},{6,7},{7,6},{8,9},{9,8},{10,11... | collective-permute-start | bytes 25165832 | tf_op jit(solution)/shard_map/ppermute | solution.py:212
  22.9 1.3 %collective-permute-start = (bf16[32,4,512]{2,1,0:T(4,128)(2,1)S(1)}, bf16[32,4,512]{2,1,0:T(4,128)(2,1)S(1)}, u32[]{:S(2)}, u32[]{:S(2)}) collective-permute-start(bf16[32,4,512]{2,1,0:T(4,128)(2,1)S(1)} %all_to_all.10.own_ref), channel_id=1, source_target_pairs={{0,1},{1,0},{2,3},{3,2},{4,5},{5,4},{6,7},{7,6},{8,9},{9,8},{10,11... | collective-permute-start | bytes 393224 | tf_op jit(solution)/shard_map/ppermute | solution.py:217
  27.8 1.4 %collective-permute-start.2 = (f32[328,128]{1,0:T(8,128)S(1)}, f32[328,128]{1,0:T(8,128)S(1)}, u32[]{:S(2)}, u32[]{:S(2)}) collective-permute-start(f32[328,128]{1,0:T(8,128)S(1)} %get-tuple-element.15.pack_ref), channel_id=1, source_target_pairs={{0,1},{1,0},{2,3},{3,2},{4,5},{5,4},{6,7},{7,6},{8,9},{9,8},{10,11... | collective-permute-start | bytes 503816 | tf_op jit(solution)/shard_map/ppermute | solution.py:247

commit v5 on v4

--- a/solution.py
+++ b/solution.py
@@ -82,17 +82,12 @@
     def scores(c):
         return dot(picked[c * CAP : (c + 1) * CAP], leaves_ref[c], 1, 1)
 
-    ms, ls, accs = [], [], []
-    s = scores(0)
-    for c in range(count):
-        z = s * scale
-        if c + 1 < count:
-            s = scores(c + 1)
-        m = jnp.max(z, axis=1, keepdims=True)
-        w = jnp.exp(z - m)
-        ms.append(m)
-        ls.append(jnp.sum(w, axis=1, keepdims=True))
-        accs.append(dot(w.astype(BF16), leaves_ref[c], 1, 0))
+    z = jnp.concatenate([scores(c) for c in range(count)], axis=0) * scale
+    m = jnp.max(z, axis=1, keepdims=True)
+    w = jnp.exp(z - m)
+    l = jnp.sum(w, axis=1, keepdims=True)
+    w = w.astype(BF16)
+    accs = [dot(w[c * CAP : (c + 1) * CAP], leaves_ref[c], 1, 0) for c in range(count)]
     info_ref[...] = cs[:, :half]
     slots = count * CAP
     for c in range(count):
@@ -101,7 +96,7 @@
     lane = lax.broadcasted_iota(jnp.int32, (slots, LANES), 1)
     base = width // LANES * slots
     pack_ref[base : base + slots] = jnp.where(
-        lane == 0, jnp.concatenate(ms, axis=0), jnp.concatenate(ls, axis=0)
+        lane == 0, m, l
     )
     pack_ref[base + slots :] = cs[:, half:]
 

time: 46.8 us -> 46.7 us (level)
  no operation moved by 1% of the time
where the time goes in v5:
time: 46.7 us; the launch traced here: 45.9 us
  blocking collectives  36.4 us (78%)
  Pallas kernels  6.32 us (14%)
  waiting for transfers between devices  1.32 us (3%)
  local copies, waits for them, and re-layouts  0.72 us (2%)
  between operations  0.67 us (1%)
    all_to_all x1, blocking collectives, per_device(): own = lax.all_to_all(spread, 'cluster', 0, 0, axis_index_groups=sides)  21.4 us
    all_to_all x1, blocking collectives, per_device(): lax.all_to_all(packed, 'cluster', 0, 0, axis_index_groups=sides, tiled=True)  15 us
    pallas_call x1, Pallas kernels, per_device(): pl.pallas_call(functools.partial(leaf_kernel, scale), out_shape=(jax.Shap...  3.56 us
    pallas_call x1, Pallas kernels, per_device(): pl.pallas_call(table_kernel, out_shape=(jax.ShapeDtypeStruct((slots, tota...  1.11 us
    ppermute x1, waiting for transfers between devices, per_device(): theirs = lax.ppermute(pack, 'cluster', swap)  1.1 us
  transfers between devices with their start and end apart: 3, of which 2 were waited for; matrix products, arithmetic and copies ran while one was open for 2% of the time, Pallas kernels for 2%

profile of v5, /device:TPU:32, one launch (start us, length us, event | category | flops | bytes accessed | tf_op | source)
XLA Modules:
  0.0 45.9 jit_solution(3271809948225137590)
XLA Ops:
  0.6 0.1 collective-permute-start.1
  0.7 0.7 %broadcast_in_dim.2 = bf16[32,4,512]{2,1,0:T(4,128)(2,1)S(1)} broadcast(bf16[4,512]{1,0:T(4,128)(2,1)} %param.4), dimensions={1,2} | broadcast | bytes 135168 | tf_op jit(solution)/shard_map/broadcast_in_dim | solution.py:209
  1.5 21.4 %all_to_all.10.own_ref = bf16[32,4,512]{2,1,0:T(4,128)(2,1)S(1)} all-to-all(bf16[32,4,512]{2,1,0:T(4,128)(2,1)S(1)} %broadcast_in_dim.2), channel_id=1, replica_groups={{0,2,4,6,8,10,12,14,16,18,20,22,24,26,28,30,32,34,36,38,40,42,44,46,48,..., dimensions={0} | all-to-all | bytes 262144 | tf_op jit(solution)/shard_map/all_to_all | solution.py:210
  22.9 0.0 collective-permute-start
  22.9 1.1 %table.1 = (bf16[64,256]{1,0:T(8,128)(2,1)S(1)}, bf16[128,128]{1,0:T(8,128)(2,1)S(1)}, bf16[128,256]{1,0:T(8,128)(2,1)S(1)}, s32[8,128]{1,0:T(8,128)S(1)}, bf16[8,512]{1,0:T(8,128)(2,1)S(1)}) custom-call(s32[8,256]{1,0:T(8,128)} %bitcast.1, bf16[8,512]{1,0:T(8,128)(2,1)} %cent_ref.1), custom_call_target="tpu_custom_call" | custom-call | flops 50000000 | bytes 4194304 | tf_op jit(solution)/shard_map/table/pallas_call | solution.py:214
  24.0 0.2 collective-permute-done.other_ref
  24.2 0.0 collective-permute-done.1.leaves_ref
  24.2 3.6 %leaf.1 = (f32[328,128]{1,0:T(8,128)S(1)}, f32[8,128]{1,0:T(8,128)S(1)}) custom-call(bf16[32,4,512]{2,1,0:T(4,128)(2,1)S(1)} %all_to_all.10.own_ref, bf16[32,4,512]{2,1,0:T(4,128)(2,1)S(1)} %collective-permute-done.other_ref, bf16[64,256]{1,0:T(8,128)(2,1)S(1)} %get-tuple-element.13.disp_ref, bf16[8,512]{1,0:T(8,128)(2,1)S(1)} %get-tuple-element.14.cent_ref, ...), custom_call_target="tpu_custom_call" | custom-call | tf_op jit(solution)/shard_map/leaf/pallas_call | solution.py:230
  27.8 0.3 collective-permute-start.2
  28.1 1.1 %collective-permute-done.2.theirs_ref = f32[328,128]{1,0:T(8,128)S(1)} collective-permute-done((f32[328,128]{1,0:T(8,128)S(1)}, f32[328,128]{1,0:T(8,128)S(1)}, u32[]{:S(2)}, u32[]{:S(2)}) %collective-permute-start.2) | collective-permute-done | bytes 167968 | tf_op jit(solution)/shard_map/ppermute | solution.py:242
  29.2 0.7 %merge.1 = f32[160,4,128]{2,1,0:T(4,128)S(1)} custom-call(f32[328,128]{1,0:T(8,128)S(1)} %get-tuple-element.15.pack_ref, f32[8,128]{1,0:T(8,128)S(1)} %get-tuple-element.16.info_ref, f32[328,128]{1,0:T(8,128)S(1)} %collective-permute-done.2.theirs_ref, bf16[128,128]{1,0:T(8,128)(2,1)S(1)} %get-tuple-element.17.mine_ref, ...), custom_call_target="tpu_custom_call" | custom-call | tf_op jit(solution)/shard_map/merge/pallas_call | solution.py:244
  29.9 0.1 convert_element_type.6
  30.0 15.0 %all_to_all.11 = f16[160,4,128]{2,1,0:T(4,128)(2,1)S(1)} all-to-all(f16[160,4,128]{2,1,0:T(4,128)(2,1)S(1)} %convert_element_type.6), channel_id=1, replica_groups={{0,2,4,6,8,10,12,14,16,18,20,22,24,26,28,30,32,34,36,38,40,42,44,46,48,..., dimensions={0} | all-to-all | bytes 327680 | tf_op jit(solution)/shard_map/all_to_all | solution.py:253
  45.0 0.1 convert_element_type.7.got_ref
  45.0 0.9 %home.1 = (bf16[4,512]{1,0:T(4,128)(2,1)}, f32[4,8]{1,0:T(4,128)}) custom-call(f32[160,4,128]{2,1,0:T(4,128)S(1)} %convert_element_type.7.got_ref), custom_call_target="tpu_custom_call" | custom-call | tf_op jit(solution)/shard_map/home/pallas_call | solution.py:254
Async XLA Ops:
  0.6 23.6 %collective-permute-start.1 = (bf16[8,1024,512]{2,1,0:T(8,128)(2,1)}, bf16[8,1024,512]{2,1,0:T(8,128)(2,1)S(1)}, u32[]{:S(2)}, u32[]{:S(2)}) collective-permute-start(bf16[8,1024,512]{2,1,0:T(8,128)(2,1)} %param.6), channel_id=1, source_target_pairs={{0,1},{1,0},{2,3},{3,2},{4,5},{5,4},{6,7},{7,6},{8,9},{9,8},{10,11... | collective-permute-start | bytes 25165832 | tf_op jit(solution)/shard_map/ppermute | solution.py:207
  22.9 1.3 %collective-permute-start = (bf16[32,4,512]{2,1,0:T(4,128)(2,1)S(1)}, bf16[32,4,512]{2,1,0:T(4,128)(2,1)S(1)}, u32[]{:S(2)}, u32[]{:S(2)}) collective-permute-start(bf16[32,4,512]{2,1,0:T(4,128)(2,1)S(1)} %all_to_all.10.own_ref), channel_id=1, source_target_pairs={{0,1},{1,0},{2,3},{3,2},{4,5},{5,4},{6,7},{7,6},{8,9},{9,8},{10,11... | collective-permute-start | bytes 393224 | tf_op jit(solution)/shard_map/ppermute | solution.py:212
  27.8 1.4 %collective-permute-start.2 = (f32[328,128]{1,0:T(8,128)S(1)}, f32[328,128]{1,0:T(8,128)S(1)}, u32[]{:S(2)}, u32[]{:S(2)}) collective-permute-start(f32[328,128]{1,0:T(8,128)S(1)} %get-tuple-element.15.pack_ref), channel_id=1, source_target_pairs={{0,1},{1,0},{2,3},{3,2},{4,5},{5,4},{6,7},{7,6},{8,9},{9,8},{10,11... | collective-permute-start | bytes 503816 | tf_op jit(solution)/shard_map/ppermute | solution.py:242
